TPU v7x, 32 devices: a whole 2x2x4 slice. The times are simulated.
32 devices in a mesh: section: 2 (over core), dp: 16 (over z, y, x).
Axes of the slice: x: 2, y: 2, z: 4, core: 2. Of those that a mesh axis runs over, the one named last changes fastest.
Arguments:
- audio_in: bfloat16 [2, 16, 96, 1024], P(None, 'dp'), may hold values from -6 to 6
- out_grad: bfloat16 [2, 16, 96, 1024], P(None, 'dp'), may hold values from -6 to 6
- item_len: int32 [2, 16], P(None, 'dp'), may hold values from 24 to 96, as said below
- rel_bucket: int32 [96], replicated, may hold values from 0 to 31, as said below
- w_qkv: float32 [2, 1024, 3072], P('section', 'dp'), may hold values from -0.1875 to 0.1875
- w_out: float32 [2, 1024, 1024], P('section', 'dp'), may hold values from -0.625 to 0.625
- w_up: float32 [2, 1024, 4096], P('section', 'dp'), may hold values from -0.1875 to 0.1875
- w_down: float32 [2, 4096, 1024], P('section', 'dp'), may hold values from -0.09375 to 0.09375
- ln1_gain: float32 [2, 1024], P('section', 'dp'), may hold values from 0.1 to 1.9
- ln1_bias: float32 [2, 1024], P('section', 'dp'), may hold values from -3 to 3
- ln2_gain: float32 [2, 1024], P('section', 'dp'), may hold values from 0.1 to 1.9
- ln2_bias: float32 [2, 1024], P('section', 'dp'), may hold values from -3 to 3
- b_out: float32 [2, 1024], P('section', 'dp'), may hold values from -3 to 3
- b_up: float32 [2, 4096], P('section', 'dp'), may hold values from -3 to 3
- b_down: float32 [2, 1024], P('section', 'dp'), may hold values from -3 to 3
- rel_table: float32 [2, 512], P('section', 'dp'), may hold values from -4 to 4
Outputs:
- layer_outputs: bfloat16 [2, 2, 16, 96, 1024], P('section', None, 'dp')
- input_grads: float32 [2, 2, 16, 96, 1024], P('section', None, 'dp')
- grad_w_qkv: float32 [2, 1024, 3072], P('section', 'dp')
- grad_w_out: float32 [2, 1024, 1024], P('section', 'dp')
- grad_w_up: float32 [2, 1024, 4096], P('section', 'dp')
- grad_w_down: float32 [2, 4096, 1024], P('section', 'dp')
- grad_ln1_gain: float32 [2, 1024], P('section', 'dp')
- grad_ln1_bias: float32 [2, 1024], P('section', 'dp')
- grad_ln2_gain: float32 [2, 1024], P('section', 'dp')
- grad_ln2_bias: float32 [2, 1024], P('section', 'dp')
- grad_b_out: float32 [2, 1024], P('section', 'dp')
- grad_b_up: float32 [2, 4096], P('section', 'dp')
- grad_b_down: float32 [2, 1024], P('section', 'dp')
- grad_rel_table: float32 [2, 512], P('section', 'dp')
Inputs may be any that keep to these rules, and one draw needn't show every extreme that they name: `item_len`: an item with more than 48 tokens is in the long bucket, else in the short one. Some item has 96 tokens and some 96/4. `rel_bucket`: entry d is the bucket of a key d positions before its query: equal to d for d < 16, never falling, each bucket used.
All inputs are finite; a program needn't handle non-finite values.
Results may differ from a plain program's by a relative error of at most 0.015.
The roundings to bfloat16 on the way count: a program that leaves them out, or rounds other values in their place, can miss the bound.
Values may be sent and summed in bfloat16 or wider, within the bound.
A program may use at most 256 MiB of HBM per device.

v0:
```python
import jax
import jax.numpy as jnp
from jax import lax
from jax.sharding import PartitionSpec as P

H = 16
NB = 32


epsilon = 1e-05
highest = lax.Precision.HIGHEST


def passed_along(block, axis, distance):
    devices = range(lax.axis_size(axis))
    route = [(i - distance, i) for i in devices if i - distance in devices]
    return lax.ppermute(block, axis, route)


def norm_rows(values):
    centre = values - jnp.mean(values, axis=-1, keepdims=True)
    return centre * lax.rsqrt(jnp.mean(centre * centre, axis=-1, keepdims=True) + epsilon)


def norm_affine(values, gain, shift):
    return norm_rows(values) * gain + shift


def contract_rows(left, right):
    return lax.dot_general(
        left, right, (((0,), (0,)), ((), ())), preferred_element_type=jnp.float32
    )


def contract_cols(left, right):
    return lax.dot_general(
        left, right, (((1,), (1,)), ((), ())), preferred_element_type=jnp.float32
    )


def toeplitz_rows(values):
    heads, length = values.shape
    reverse = jnp.flip(values, axis=1)
    padded = jnp.concatenate([reverse, jnp.zeros_like(reverse)], axis=1)
    tiled = jnp.tile(padded, (1, length))[:, : length * (2 * length - 1)]
    return tiled.reshape(heads, length, 2 * length - 1)[:, :, length - 1 :]


def diagonal_sums(grid):
    heads, length, _ = grid.shape
    widened = jnp.concatenate([jnp.zeros((heads, length, length - 1), grid.dtype), grid], axis=2)
    flat = widened.reshape(heads, length * (2 * length - 1))
    flat = jnp.concatenate([flat, jnp.zeros((heads, length), grid.dtype)], axis=1)
    folded = jnp.sum(flat.reshape(heads, length, 2 * length), axis=1)
    return jnp.flip(folded[:, :length], axis=1)


def bucket_table(buckets):
    return (buckets[None, :] == jnp.arange(NB, dtype=jnp.int32)[:, None]).astype(jnp.float32)


def make_bias(table_flat, onehot):
    table = table_flat.astype(jnp.float32).reshape(NB, H)
    per_distance = jnp.dot(table.T, onehot, precision=highest)
    return toeplitz_rows(per_distance)


def weight_terms(factors):
    normed, d_qkv, mixed, d_attn, second, d_hidden, activated, d_branch = factors
    return (
        contract_rows(normed, d_qkv),
        contract_rows(mixed, d_attn),
        contract_rows(second, d_hidden),
        contract_rows(activated, d_branch),
    )


def forward_item(inputs, length, bias, weights):
    (
        w_qkv,
        w_out,
        w_up,
        w_down,
        gain_one,
        shift_one,
        gain_two,
        shift_two,
        bias_out,
        bias_up,
        bias_down,
    ) = weights
    rows, width = inputs.shape
    heads = bias.shape[0]
    head_dim = width // heads
    scale = head_dim ** (-0.5)
    position = jnp.arange(rows)
    visible = (position[None, :] <= position[:, None])[None] & (position[None, None, :] < length)
    valid = (position < length).astype(jnp.float32)[:, None]
    normed = norm_affine(
        inputs, gain_one.astype(jnp.float32), shift_one.astype(jnp.float32)
    ).astype(jnp.bfloat16)
    qkv = jnp.dot(normed, w_qkv, preferred_element_type=jnp.float32).astype(jnp.bfloat16)
    query = qkv[:, :width].reshape(rows, heads, head_dim)
    keys = qkv[:, width : 2 * width].reshape(rows, heads, head_dim)
    values = qkv[:, 2 * width :].reshape(rows, heads, head_dim)
    scores = (
        jnp.einsum("ihd,jhd->hij", query, keys, preferred_element_type=jnp.float32) * scale + bias
    )
    scores = jnp.where(visible, scores, -1000000000.0)
    raised = jnp.exp(scores - jnp.max(scores, axis=-1, keepdims=True))
    probs = raised / jnp.sum(raised, axis=-1, keepdims=True)
    probs_low = probs.astype(jnp.bfloat16)
    mixed = (
        jnp.einsum("hij,jhd->ihd", probs_low, values, preferred_element_type=jnp.float32)
        .reshape(rows, width)
        .astype(jnp.bfloat16)
    )
    middle = (
        inputs
        + jnp.dot(mixed, w_out, preferred_element_type=jnp.float32)
        + bias_out.astype(jnp.float32)
    )
    second = norm_affine(
        middle, gain_two.astype(jnp.float32), shift_two.astype(jnp.float32)
    ).astype(jnp.bfloat16)
    hidden = jnp.dot(second, w_up, preferred_element_type=jnp.float32) + bias_up.astype(jnp.float32)
    activated = jax.nn.gelu(hidden).astype(jnp.bfloat16)
    result = (
        middle
        + jnp.dot(activated, w_down, preferred_element_type=jnp.float32)
        + bias_down.astype(jnp.float32)
    ) * valid
    saved = (
        normed,
        query,
        keys,
        values,
        probs,
        probs_low,
        mixed,
        middle,
        second,
        hidden,
        activated,
        valid,
    )
    return (result, saved)


def backward_item(inputs, length, bias, weights, upstream, onehot):
    (
        w_qkv,
        w_out,
        w_up,
        w_down,
        gain_one,
        shift_one,
        gain_two,
        shift_two,
        bias_out,
        bias_up,
        bias_down,
    ) = weights
    _, saved = forward_item(inputs, length, bias, weights)
    (
        normed,
        query,
        keys,
        values,
        probs,
        probs_low,
        mixed,
        middle,
        second,
        hidden,
        activated,
        valid,
    ) = saved
    rows, width = inputs.shape
    heads = bias.shape[0]
    head_dim = width // heads
    scale = head_dim ** (-0.5)
    direct = upstream * valid
    d_branch = direct.astype(jnp.bfloat16)
    grad_bdown = jnp.sum(d_branch.astype(jnp.float32), axis=0)
    d_activated = contract_cols(d_branch, w_down)
    _, gelu_back = jax.vjp(jax.nn.gelu, hidden)
    d_hidden = gelu_back(d_activated)[0].astype(jnp.bfloat16)
    grad_bup = jnp.sum(d_hidden.astype(jnp.float32), axis=0)
    d_second = contract_cols(d_hidden, w_up)
    _, second_back = jax.vjp(
        norm_affine, middle, gain_two.astype(jnp.float32), shift_two.astype(jnp.float32)
    )
    d_middle, grad_gain_two, grad_shift_two = second_back(d_second)
    d_middle = d_middle + direct
    d_attn = d_middle.astype(jnp.bfloat16)
    grad_bout = jnp.sum(d_attn.astype(jnp.float32), axis=0)
    d_mixed = contract_cols(d_attn, w_out).astype(jnp.bfloat16).reshape(rows, heads, head_dim)
    grad_values = jnp.einsum("hij,ihd->jhd", probs_low, d_mixed, preferred_element_type=jnp.float32)
    d_probs = jnp.einsum("ihd,jhd->hij", d_mixed, values, preferred_element_type=jnp.float32)
    d_scores = (probs * (d_probs - jnp.sum(probs * d_probs, axis=-1, keepdims=True))).astype(
        jnp.bfloat16
    )
    grad_query = (
        jnp.einsum("hij,jhd->ihd", d_scores, keys, preferred_element_type=jnp.float32) * scale
    )
    grad_keys = (
        jnp.einsum("hij,ihd->jhd", d_scores, query, preferred_element_type=jnp.float32) * scale
    )
    d_qkv = jnp.concatenate(
        [
            grad_query.reshape(rows, width),
            grad_keys.reshape(rows, width),
            grad_values.reshape(rows, width),
        ],
        axis=1,
    ).astype(jnp.bfloat16)
    d_normed = contract_cols(d_qkv, w_qkv)
    _, first_back = jax.vjp(
        norm_affine, inputs, gain_one.astype(jnp.float32), shift_one.astype(jnp.float32)
    )
    d_inputs, grad_gain_one, grad_shift_one = first_back(d_normed)
    d_inputs = d_inputs + d_middle
    per_distance = diagonal_sums(d_scores.astype(jnp.float32))
    grad_table = jnp.dot(onehot, per_distance.T, precision=highest).reshape(-1)
    factors = (normed, d_qkv, mixed, d_attn, second, d_hidden, activated, d_branch)
    small = (
        grad_gain_one,
        grad_shift_one,
        grad_gain_two,
        grad_shift_two,
        grad_bout,
        grad_bup,
        grad_bdown,
        grad_table,
    )
    return (d_inputs, factors, small)


def local(
    audio_in,
    out_grad,
    item_len,
    rel_bucket,
    w_qkv,
    w_out,
    w_up,
    w_down,
    ln1_gain,
    ln1_bias,
    ln2_gain,
    ln2_bias,
    b_out,
    b_up,
    b_down,
    rel_table,
):
    section = lax.axis_index("section")
    micro = audio_in.shape[0]
    rows = audio_in.shape[2]
    width = audio_in.shape[3]
    qkv_part = w_qkv[0].astype(jnp.bfloat16)
    out_part = w_out[0].astype(jnp.bfloat16)
    up_part = w_up[0].astype(jnp.bfloat16)
    down_part = w_down[0].astype(jnp.bfloat16)
    gain_one_part = ln1_gain[0].astype(jnp.bfloat16)
    shift_one_part = ln1_bias[0].astype(jnp.bfloat16)
    gain_two_part = ln2_gain[0].astype(jnp.bfloat16)
    shift_two_part = ln2_bias[0].astype(jnp.bfloat16)
    bias_out_part = b_out[0].astype(jnp.bfloat16)
    bias_up_part = b_up[0].astype(jnp.bfloat16)
    bias_down_part = b_down[0].astype(jnp.bfloat16)
    table_part = rel_table[0].astype(jnp.bfloat16)
    parts = (
        qkv_part,
        out_part,
        up_part,
        down_part,
        gain_one_part,
        shift_one_part,
        gain_two_part,
        shift_two_part,
        bias_out_part,
        bias_up_part,
        bias_down_part,
        table_part,
    )
    gathered = (
        lax.all_gather(qkv_part, "dp", axis=0, tiled=True),
        lax.all_gather(out_part, "dp", axis=0, tiled=True),
        lax.all_gather(up_part, "dp", axis=0, tiled=True),
        lax.all_gather(down_part, "dp", axis=0, tiled=True),
        lax.all_gather(gain_one_part, "dp", axis=0, tiled=True),
        lax.all_gather(shift_one_part, "dp", axis=0, tiled=True),
        lax.all_gather(gain_two_part, "dp", axis=0, tiled=True),
        lax.all_gather(shift_two_part, "dp", axis=0, tiled=True),
        lax.all_gather(bias_out_part, "dp", axis=0, tiled=True),
        lax.all_gather(bias_up_part, "dp", axis=0, tiled=True),
        lax.all_gather(bias_down_part, "dp", axis=0, tiled=True),
        lax.all_gather(table_part, "dp", axis=0, tiled=True),
    )
    onehot = bucket_table(rel_bucket)
    weights = gathered[:11]
    bias = make_bias(gathered[11], onehot)
    lengths = item_len[:, 0]
    hidden_width = gathered[2].shape[1]

    def run_forward(layer_in, length):
        return forward_item(layer_in.astype(jnp.float32), length, bias, weights)[0]

    def skip_forward(layer_in, length):
        return jnp.zeros(layer_in.shape, jnp.float32)

    incoming = jnp.zeros((rows, width), jnp.bfloat16)
    produced = []
    taken = []
    for tick in range(micro + 1):
        slot = tick - section
        active = jnp.logical_and(slot >= 0, slot < micro)
        length = lengths[jnp.clip(slot, 0, micro - 1)]
        own = audio_in[min(tick, micro - 1), 0]
        layer_in = jnp.where(section == 0, own, incoming)
        layer_out = lax.cond(active, run_forward, skip_forward, layer_in, length).astype(
            jnp.bfloat16
        )
        produced.append(layer_out)
        taken.append(layer_in)
        if tick < micro:
            incoming = passed_along(layer_out, "section", 1)
    outputs = jnp.stack(
        [jnp.where(section == 0, produced[batch], produced[batch + 1]) for batch in range(micro)]
    )
    kept = jnp.stack(
        [jnp.where(section == 0, taken[batch], taken[batch + 1]) for batch in range(micro)]
    )
    regathered = (
        lax.all_gather(qkv_part, "dp", axis=0, tiled=True),
        lax.all_gather(out_part, "dp", axis=0, tiled=True),
        lax.all_gather(up_part, "dp", axis=0, tiled=True),
        lax.all_gather(down_part, "dp", axis=0, tiled=True),
        lax.all_gather(gain_one_part, "dp", axis=0, tiled=True),
        lax.all_gather(shift_one_part, "dp", axis=0, tiled=True),
        lax.all_gather(gain_two_part, "dp", axis=0, tiled=True),
        lax.all_gather(shift_two_part, "dp", axis=0, tiled=True),
        lax.all_gather(bias_out_part, "dp", axis=0, tiled=True),
        lax.all_gather(bias_up_part, "dp", axis=0, tiled=True),
        lax.all_gather(bias_down_part, "dp", axis=0, tiled=True),
        lax.all_gather(table_part, "dp", axis=0, tiled=True),
    )
    back_weights = regathered[:11]
    back_bias = make_bias(regathered[11], onehot)

    def run_backward(layer_in, length, upstream):
        return backward_item(
            layer_in.astype(jnp.float32), length, back_bias, back_weights, upstream, onehot
        )

    def skip_backward(layer_in, length, upstream):
        zero_rows = jnp.zeros((rows, width), jnp.bfloat16)
        zero_triple = jnp.zeros((rows, 3 * width), jnp.bfloat16)
        zero_hidden = jnp.zeros((rows, hidden_width), jnp.bfloat16)
        factors = (
            zero_rows,
            zero_triple,
            zero_rows,
            zero_rows,
            zero_rows,
            zero_hidden,
            zero_hidden,
            zero_rows,
        )
        small = tuple((jnp.zeros(piece.shape, jnp.float32) for piece in gathered[4:]))
        return (jnp.zeros(upstream.shape, jnp.float32), factors, small)

    small_totals = tuple((jnp.zeros(piece.shape, jnp.float32) for piece in gathered[4:]))
    shares = tuple((jnp.zeros(piece.shape, jnp.float32) for piece in parts))
    returned = jnp.zeros((rows, width), jnp.bfloat16)
    results = []
    sent_list = []
    factor_list = []
    for tick in range(micro + 1):
        slot = tick - 1 + section
        active = jnp.logical_and(slot >= 0, slot < micro)
        pick = jnp.clip(slot, 0, micro - 1)
        length = lengths[pick]
        layer_in = kept[pick]
        target = out_grad[min(tick, micro - 1), 0].astype(jnp.float32)
        upstream = jnp.where(section == 1, target, returned.astype(jnp.float32))
        d_inputs, factors, small = lax.cond(
            active, run_backward, skip_backward, layer_in, length, upstream
        )
        factor_list.append(factors)
        small_totals = tuple((total + term for total, term in zip(small_totals, small)))
        results.append(d_inputs)
        if tick < micro:
            sent = d_inputs.astype(jnp.bfloat16)
            sent_list.append(lax.optimization_barrier(sent))
            returned = passed_along(sent, "section", -1)
    stacked = tuple(
        (jnp.concatenate([entry[index] for entry in factor_list], axis=0) for index in range(8))
    )
    totals = weight_terms(stacked) + small_totals
    shares = (
        lax.psum_scatter(totals[0], "dp", scatter_dimension=0, tiled=True),
        lax.psum_scatter(totals[1], "dp", scatter_dimension=0, tiled=True),
        lax.psum_scatter(totals[2], "dp", scatter_dimension=0, tiled=True),
        lax.psum_scatter(totals[3], "dp", scatter_dimension=0, tiled=True),
        lax.psum_scatter(totals[4], "dp", scatter_dimension=0, tiled=True),
        lax.psum_scatter(totals[5], "dp", scatter_dimension=0, tiled=True),
        lax.psum_scatter(totals[6], "dp", scatter_dimension=0, tiled=True),
        lax.psum_scatter(totals[7], "dp", scatter_dimension=0, tiled=True),
        lax.psum_scatter(totals[8], "dp", scatter_dimension=0, tiled=True),
        lax.psum_scatter(totals[9], "dp", scatter_dimension=0, tiled=True),
        lax.psum_scatter(totals[10], "dp", scatter_dimension=0, tiled=True),
        lax.psum_scatter(totals[11], "dp", scatter_dimension=0, tiled=True),
    )
    input_grads = jnp.stack(
        [
            jnp.where(section == 0, results[batch + 1], sent_list[batch].astype(jnp.float32))
            for batch in range(micro)
        ]
    )
    grads_out = tuple((share[None] for share in shares))
    return (outputs[None, :, None], input_grads[None, :, None]) + grads_out


def solution(mesh):
    return jax.shard_map(
        local,
        mesh=mesh,
        in_specs=(
            P(None, "dp", None, None),
            P(None, "dp", None, None),
            P(None, "dp"),
            P(),
            P("section", "dp", None),
            P("section", "dp", None),
            P("section", "dp", None),
            P("section", "dp", None),
            P("section", "dp"),
            P("section", "dp"),
            P("section", "dp"),
            P("section", "dp"),
            P("section", "dp"),
            P("section", "dp"),
            P("section", "dp"),
            P("section", "dp"),
        ),
        out_specs=(
            P("section", None, "dp", None, None),
            P("section", None, "dp", None, None),
            P("section", "dp", None),
            P("section", "dp", None),
            P("section", "dp", None),
            P("section", "dp", None),
            P("section", "dp"),
            P("section", "dp"),
            P("section", "dp"),
            P("section", "dp"),
            P("section", "dp"),
            P("section", "dp"),
            P("section", "dp"),
            P("section", "dp"),
        ),
        check_vma=False,
    )
```

profile of v0, /device:TPU:0, one launch (start us, length us, event | category | flops | bytes accessed | tf_op | source)
XLA Modules:
  0.0 1668.4 jit_solution(18019151921288245632)
XLA Ops:
  9.0 2.0 convert_element_type.770
  16.8 79.0 %all-reduce.23 = (bf16[1024]{0:T(1024)(128)(2,1)S(1)}, bf16[1024]{0:T(1024)(128)(2,1)S(1)}, bf16[512]{0:T(512)(128)(2,1)S(1)}, bf16[1024]{0:T(1024)(128)(2,1)S(1...) all-reduce(bf16[1024]{0:T(1024)(128)(2,1)S(1)} %dynamic-update-slic, ...), channel_id=2, replica_groups=mesh['section'=2,'dp'=16] {'dp'}, use_global_device_ids=true, to_apply=%add.7 | all-reduce | flops 6656 | bytes 26624 | tf_op jit(solution)/shard_map/all_gather | solution.py:293
  97.9 3.4 reshape.865
  101.7 35.9 %all-gather.9 = bf16[1,4096]{1,0:T(2,128)(2,1)S(1)} all-gather(bf16[1,256]{1,0:T(2,128)(2,1)S(1)} %convert_element_type.784), channel_id=11, replica_groups=mesh['section'=2,'dp'=16] {'dp'}, dimensions={1}, use_global_device_ids=true | all-gather | bytes 8704 | tf_op jit(solution)/shard_map/all_gather | solution.py:298
  137.7 34.0 %all-gather.17.cloned.1.call-done = bf16[1,1024,3072]{2,1,0:T(8,128)(2,1)} async-done(((bf16[1,64,3072]{2,1,0:T(8,128)(2,1)}), bf16[1,1024,3072]{2,1,0:T(8,128)(2,1)}) %all-gather.17.cloned.1.call-update) | async-done | bytes 6291472 | tf_op jit(solution)/shard_map/all_gather | solution.py:289
  171.7 114.5 %all-gather.21.cloned.1.call-done = bf16[1,1024,4096]{2,1,0:T(8,128)(2,1)} async-done(((bf16[1,64,4096]{2,1,0:T(8,128)(2,1)}), bf16[1,1024,4096]{2,1,0:T(8,128)(2,1)}) %all-gather.21.cloned.1.call-update) | async-done | bytes 8388624 | tf_op jit(solution)/shard_map/all_gather | solution.py:291
  286.2 114.3 %all-gather.23.cloned.1.call-done = bf16[1,4096,1024]{2,1,0:T(8,128)(2,1)} async-done(((bf16[1,256,1024]{2,1,0:T(8,128)(2,1)}), bf16[1,4096,1024]{2,1,0:T(8,128)(2,1)}) %all-gather.23.cloned.1.call-update) | async-done | bytes 8388624 | tf_op jit(solution)/shard_map/all_gather | solution.py:292
  400.5 24.0 %conditional.6 = (bf16[96,1024]{1,0:T(8,128)(2,1)S(1)}) conditional(s32[]{:T(128)} %convert_element_type.765, () %tuple.78, (bf16[96,1024]{1,0:T(8,128)(2,1)S(1)}, bf16[1024]{0:T(1024)(128)(2,1)S(1)}, bf16[1024]{0:T(1024)(128)(2,1)S(1)}, bf16[1024,3072]{1,0:T(8,128)(2,1)}, s32[]{:T(128)}, /*index=5*/s32[2,1]{0,1:T(1,128)S(1)}, ...), branch_computations={%region_0.1_spmd, %region_1.8_spmd} | conditional | flops 2461956096 | bytes 47279484 | solution.py:323
  403.2 4.0 convolution_convert_fusion
  410.2 2.6 convolution_convert_fusion.1
  415.4 9.1 fusion.16
  427.6 25.7 %conditional.7 = (bf16[96,1024]{1,0:T(8,128)(2,1)S(1)}) conditional(s32[]{:T(128)} %convert_element_type.790, () %tuple.80, (bf16[96,1024]{1,0:T(8,128)(2,1)S(1)}, bf16[1024]{0:T(1024)(128)(2,1)S(1)}, bf16[1024]{0:T(1024)(128)(2,1)S(1)}, bf16[1024,3072]{1,0:T(8,128)(2,1)}, s32[]{:T(128)}, /*index=5*/s32[2,1]{0,1:T(1,128)}, ...), branch_computations={%region_8.9_spmd, %region_9.16_spmd} | conditional | flops 2461956096 | bytes 47394284 | solution.py:323
  432.8 4.0 convolution_convert_fusion.2
  440.4 1.9 convolution_convert_fusion.3
  444.2 9.1 fusion.59
  453.4 2.4 collective-permute-start.1
  459.5 19.3 %conditional.9 = (bf16[96,1024]{1,0:T(8,128)(2,1)}, bf16[96,3072]{0,1:T(8,128)(2,1)}, bf16[96,1024]{0,1:T(8,128)(2,1)}, bf16[96,1024]{1,0:T(8,128)(2,1)}, bf16[9...) conditional(s32[]{:T(128)} %convert_element_type.795, () %tuple.85, ...), branch_computations={%region_24.25_spmd, %region_25.45_spmd} | conditional | flops 4164568320 | bytes 155590528 | solution.py:389
  481.1 40.2 %collective-permute-done.2 = bf16[96,1024]{1,0:T(8,128)(2,1)S(1)} collective-permute-done((bf16[96,1024]{1,0:T(8,128)(2,1)}, bf16[96,1024]{1,0:T(8,128)(2,1)S(1)}, u32[]{:S(2)}, u32[]{:S(2)}) %collective-permute-start.2) | collective-permute-done | bytes 196640 | tf_op jit(solution)/shard_map/ppermute | solution.py:17
  521.3 60.3 %conditional.10 = (f32[96,1024]{1,0:T(8,128)}, bf16[96,1024]{1,0:T(8,128)(2,1)}, bf16[96,3072]{0,1:T(8,128)(2,1)}, bf16[96,1024]{0,1:T(8,128)(2,1)}, bf16[96,102...) conditional(s32[]{:T(128)} %convert_element_type.792, () %tuple.84, ...), branch_computations={%region_45.46_spmd, %region_46.66_spmd} | conditional | flops 4163880192 | bytes 155978192 | solution.py:389
  524.8 2.7 convert_reduce_fusion.9
  527.5 7.4 fusion.321
  535.7 2.1 convolution_convert_fusion.10
  540.8 2.6 convolution_convert_fusion.12
  546.2 7.7 convert_reduce_fusion.7
  553.9 4.5 multiply_reduce_fusion.8
  560.1 2.4 convolution_convert_fusion.13
  563.6 1.9 convolution_convert_fusion.11
  569.1 5.8 fusion.288
  579.1 2.0 reshape.870
  583.0 2.2 collective-permute-done.3
  585.3 61.9 %conditional.11 = (f32[96,1024]{1,0:T(8,128)}, bf16[96,1024]{1,0:T(8,128)(2,1)}, bf16[96,3072]{0,1:T(8,128)(2,1)}, bf16[96,1024]{0,1:T(8,128)(2,1)}, bf16[96,102...) conditional(s32[]{:T(128)} %convert_element_type.799, () %tuple.88, ...), branch_computations={%region_66.67_spmd, %region_67.87_spmd} | conditional | flops 4163781888 | bytes 155778432 | solution.py:389
  589.0 2.8 convert_reduce_fusion.13
  591.8 7.4 fusion.322
  599.9 2.1 convolution_convert_fusion.14
  605.2 2.6 convolution_convert_fusion.16
  610.5 8.3 convert_reduce_fusion.11
  618.8 4.5 multiply_reduce_fusion.12
  625.0 2.4 convolution_convert_fusion.17
  633.8 5.8 fusion.289
  643.7 2.0 reshape.872
  647.2 4.7 fusion.255
  651.9 10.4 fusion.237
  662.3 12.2 fusion.243
  674.8 12.1 fusion.249
  696.3 74.5 %all-reduce.22 = (f32[1024]{0:T(1024)S(1)}, f32[1024]{0:T(1024)S(1)}, f32[1024]{0:T(1024)S(1)}, f32[1024]{0:T(1024)S(1)}, f32[1024]{0:T(1024)S(1)}, /*index=5*/f...) all-reduce(f32[1024]{0:T(1024)S(1)} %get-tuple-element.1307, ...), channel_id=18, replica_groups=mesh['section'=2,'dp'=16] {'dp'}, use_global_device_ids=true, to_apply=%region_91.92.clone | all-reduce | flops 10752 | bytes 86016
  777.6 179.7 %reduce-scatter.5.cloned.1.call-done = f32[64,3072]{1,0:T(8,128)} async-done(((f32[1024,3072]{1,0:T(8,128)}), f32[64,3072]{1,0:T(8,128)}) %reduce-scatter.5.cloned.1.call-update) | async-done | bytes 786448 | tf_op jit(solution)/shard_map/reduce_scatter | solution.py:404
  957.3 349.0 %reduce-scatter.9.cloned.1.call-done = f32[64,4096]{1,0:T(8,128)} async-done(((f32[1024,4096]{1,0:T(8,128)}), f32[64,4096]{1,0:T(8,128)}) %reduce-scatter.9.cloned.1.call-update) | async-done | bytes 1048592 | tf_op jit(solution)/shard_map/reduce_scatter | solution.py:406
  1306.3 355.0 %reduce-scatter.11.cloned.1.call-done = f32[256,1024]{1,0:T(8,128)} async-done(((f32[4096,1024]{1,0:T(8,128)}), f32[256,1024]{1,0:T(8,128)}) %reduce-scatter.11.cloned.1.call-update) | async-done | bytes 1048592 | tf_op jit(solution)/shard_map/reduce_scatter | solution.py:407
  (476 shorter events, 106.8 us)
Async XLA Ops:
  7.2 130.5 %all-gather.19.cloned.1.call-start = ((), (), s32[]{:S(2)}) async-start(), calls=%async_computation.9 | async-start | bytes 2228224 | tf_op jit(solution)/shard_map/all_gather | solution.py:290
  9.0 162.7 %all-gather.17.cloned.1.call-start = ((), (), s32[]{:S(2)}) async-start(), calls=%async_computation.8 | async-start | bytes 6684672 | tf_op jit(solution)/shard_map/all_gather | solution.py:289
  11.0 275.2 %all-gather.21.cloned.1.call-start = ((), (), s32[]{:S(2)}) async-start(), calls=%async_computation.10 | async-start | bytes 8912896 | tf_op jit(solution)/shard_map/all_gather | solution.py:291
  12.0 83.9 %copy-start.112 = (s32[96]{0:T(128)S(1)}, s32[96]{0:T(128)}, u32[]{:S(2)}) copy-start(s32[96]{0:T(128)} %param.31) | copy-start | bytes 1156
  12.1 388.4 %all-gather.23.cloned.1.call-start = ((), (), s32[]{:S(2)}) async-start(), calls=%async_computation.11 | async-start | bytes 8912896 | tf_op jit(solution)/shard_map/all_gather | solution.py:292
  13.0 764.6 %reduce-scatter.7.cloned.1.call-start = ((), (), s32[]{:S(2)}) async-start(), calls=%async_computation.5 | async-start | bytes 4456448 | tf_op jit(solution)/shard_map/reduce_scatter | solution.py:405
  95.8 331.8 %copy-start.56 = (bf16[1024]{0:T(1024)(128)(2,1)}, bf16[1024]{0:T(1024)(128)(2,1)S(1)}, u32[]{:S(2)}) copy-start(bf16[1024]{0:T(1024)(128)(2,1)S(1)} %get-tuple-element.1201) | copy-start | bytes 6148
  95.8 331.8 %copy-start.58 = (bf16[1024]{0:T(1024)(128)(2,1)}, bf16[1024]{0:T(1024)(128)(2,1)S(1)}, u32[]{:S(2)}) copy-start(bf16[1024]{0:T(1024)(128)(2,1)S(1)} %get-tuple-element.1202) | copy-start | bytes 6148
  95.8 331.8 %copy-start.60 = (bf16[1024]{0:T(1024)(128)(2,1)}, bf16[1024]{0:T(1024)(128)(2,1)S(1)}, u32[]{:S(2)}) copy-start(bf16[1024]{0:T(1024)(128)(2,1)S(1)} %get-tuple-element.1203) | copy-start | bytes 6148
  95.8 331.8 %copy-start.67 = (bf16[1024]{0:T(1024)(128)(2,1)}, bf16[1024]{0:T(1024)(128)(2,1)S(1)}, u32[]{:S(2)}) copy-start(bf16[1024]{0:T(1024)(128)(2,1)S(1)} %get-tuple-element.1204) | copy-start | bytes 6148
  97.9 39.7 %copy-start.42 = (bf16[2,1,96,1024]{3,2,1,0:T(8,128)(2,1)S(1)}, bf16[2,1,96,1024]{3,2,1,0:T(8,128)(2,1)}, u32[]{:S(2)}) copy-start(bf16[2,1,96,1024]{3,2,1,0:T(8,128)(2,1)} %param.28) | copy-start | bytes 1179652
  101.4 299.1 %copy-start.128 = (s32[2,1]{0,1:T(1,128)S(1)}, s32[2,1]{0,1:T(1,128)}, u32[]{:S(2)}) copy-start(s32[2,1]{0,1:T(1,128)} %param.30) | copy-start | bytes 28
  424.5 2.4 collective-permute-start
  453.3 5.5 copy-start.50
  453.4 5.5 copy-start.57
  453.4 5.5 copy-start.59
  453.4 5.5 copy-start.61
  453.4 5.5 copy-start.129
  453.4 3.5 collective-permute-start.1
  478.8 42.5 %copy-start.94 = (f32[512]{0:T(512)}, f32[512]{0:T(512)S(1)}, u32[]{:S(2)}) copy-start(f32[512]{0:T(512)S(1)} %get-tuple-element.815) | copy-start | bytes 6148
  478.8 42.5 %copy-start.64 = (f32[4096]{0:T(1024)}, f32[4096]{0:T(1024)S(1)}, u32[]{:S(2)}) copy-start(f32[4096]{0:T(1024)S(1)} %get-tuple-element.809) | copy-start | bytes 49156
  478.8 42.5 %collective-permute-start.2 = (bf16[96,1024]{1,0:T(8,128)(2,1)}, bf16[96,1024]{1,0:T(8,128)(2,1)S(1)}, u32[]{:S(2)}, u32[]{:S(2)}) collective-permute-start(bf16[96,1024]{1,0:T(8,128)(2,1)} %get-tuple-element.766), channel_id=1, source_target_pairs={{16,0},{17,1},{18,2},{19,3},{20,4},{21,5},{22,6},{23,7},{24,8},{25... | collective-permute-start | bytes 589832 | tf_op jit(solution)/shard_map/ppermute | solution.py:17
  481.1 40.3 %copy-start.14 = (f32[96,1024]{1,0:T(8,128)}, f32[96,1024]{1,0:T(8,128)S(1)}, u32[]{:S(2)}) copy-start(f32[96,1024]{1,0:T(8,128)S(1)} %bitcast_convert_fusion) | copy-start | bytes 1179652
  524.0 10.9 copy-start.88
  524.8 10.2 copy-start.101
  524.8 10.8 slice-start.2
  527.5 8.1 slice-start.3
  545.4 8.5 slice-start.8
  546.2 7.7 slice-start.9
  569.1 5.8 copy-start.116
  569.1 5.8 copy-start.102
  569.1 6.7 copy-start.11
  569.1 6.7 copy-start.13
  581.7 3.5 collective-permute-start.3
  588.9 10.4 copy-start.103
  588.9 11.0 slice-start.4
  591.8 8.1 slice-start.5
  609.7 9.1 slice-start.10
  610.5 8.3 slice-start.11
  633.7 5.9 copy-start.118
  633.7 5.9 copy-start.104
  633.8 6.7 copy-start.18
  633.8 6.7 copy-start.20
  651.9 305.5 %reduce-scatter.5.cloned.1.call-start = ((), (), s32[]{:S(2)}) async-start(), calls=%async_computation.4 | async-start | bytes 13369344 | tf_op jit(solution)/shard_map/reduce_scatter | solution.py:404
  662.3 644.0 %reduce-scatter.9.cloned.1.call-start = ((), (), s32[]{:S(2)}) async-start(), calls=%async_computation.6 | async-start | bytes 17825792 | tf_op jit(solution)/shard_map/reduce_scatter | solution.py:406
  674.6 986.8 %reduce-scatter.11.cloned.1.call-start = ((), (), s32[]{:S(2)}) async-start(), calls=%async_computation.7 | async-start | bytes 17825792 | tf_op jit(solution)/shard_map/reduce_scatter | solution.py:407
  689.8 5.8 copy-start.63
  689.8 5.8 copy-start.65
  (73 other events, 192.8 us)
Sparse Core Ops, SparseCore 0:
  11.4 63.8 all-gather.18
  78.7 93.0 all-gather.16
  175.1 111.0 all-gather.20
  289.4 111.0 all-gather.22
  652.0 95.4 reduce-scatter.6
  753.6 203.6 reduce-scatter.4
  960.3 345.9 reduce-scatter.8
  1309.3 352.0 reduce-scatter.10
where the time goes:
time: 1680 us; the launch traced here: 1670 us
  waiting for transfers between devices  1190 us (71%)
  blocking collectives  189 us (11%)
  matrix products  148 us (9%)
  other arithmetic  52.8 us (3%)
  local copies, waits for them, and re-layouts  51.4 us (3%)
  between operations  18.5 us (1%)
    reduce_scatter x1, waiting for transfers between devices, local(): lax.psum_scatter(totals[3], 'dp', scatter_dimension=0, tiled=True)  355 us
    reduce_scatter x1, waiting for transfers between devices, local(): lax.psum_scatter(totals[2], 'dp', scatter_dimension=0, tiled=True)  349 us
    reduce_scatter x1, waiting for transfers between devices, local(): lax.psum_scatter(totals[0], 'dp', scatter_dimension=0, tiled=True)  180 us
    all_gather x1, waiting for transfers between devices, local(): lax.all_gather(up_part, 'dp', axis=0, tiled=True)  114 us
    all_gather x1, waiting for transfers between devices, local(): lax.all_gather(down_part, 'dp', axis=0, tiled=True)  114 us
    all_gather x1, blocking collectives, local(): lax.all_gather(gain_one_part, 'dp', axis=0, tiled=True)  79 us
    unnamed x1, blocking collectives  74.5 us
    ppermute x4, waiting for transfers between devices, passed_along(): return lax.ppermute(block, axis, route)  43.4 us
  transfers between devices with their start and end apart: 12, of which 10 were waited for; matrix products, arithmetic and copies ran while one was open for 4% of the time, Pallas kernels for 0%

commit v1 on v0

--- a/solution.py
+++ b/solution.py
@@ -1,6 +1,8 @@
 import jax
 import jax.numpy as jnp
 from jax import lax
+from jax.experimental import pallas as pl
+from jax.experimental.pallas import tpu as pltpu
 from jax.sharding import PartitionSpec as P
 
 H = 16
@@ -424,9 +426,690 @@
     return (outputs[None, :, None], input_grads[None, :, None]) + grads_out
 
 
+E5 = 1e-05
+F32 = jnp.float32
+BF = jnp.bfloat16
+MESH = pl.DeviceIdType.MESH
+GELU_K = 0.7978845608028654
+
+
+class Place:
+    def __init__(self):
+        self.s = lax.axis_index("section")
+        d = lax.axis_index("dp")
+        self.x = d % 2
+        self.y = (d // 2) % 2
+        self.z = (d // 4) % 2
+        self.h = d // 8
+
+    def device(self, s=None, x=None, y=None, z=None, h=None):
+        s = self.s if s is None else s
+        x = self.x if x is None else x
+        y = self.y if y is None else y
+        z = self.z if z is None else z
+        h = self.h if h is None else h
+        return (s, x + 2 * y + 4 * z + 8 * h)
+
+    def sibling(self):
+        return self.device(s=1 - self.s)
+
+    def team(self, k):
+        kx, kz = k % 2, k // 2
+        px = self.x + kx * (1 - 2 * self.x)
+        pz = self.z + kz * (1 - 2 * self.z)
+        return self.device(x=px, z=pz), px + 2 * pz
+
+    def peers(self):
+        return (
+            self.sibling(),
+            self.team(1)[0],
+            self.team(2)[0],
+            self.team(3)[0],
+            self.device(y=1 - self.y),
+            self.device(h=1 - self.h),
+        )
+
+
+def meet(peers):
+    bell = pltpu.get_barrier_semaphore()
+    for peer in peers:
+        pl.semaphore_signal(bell, inc=1, device_id=peer, device_id_type=MESH)
+    pl.semaphore_wait(bell, len(peers))
+
+
+def remote(src, dst, send, recv, device):
+    return pltpu.make_async_remote_copy(
+        src_ref=src, dst_ref=dst, send_sem=send, recv_sem=recv, device_id=device, device_id_type=MESH
+    )
+
+
+def gather_kernel(s1, w2, sp, W1, W2, SP, ls, ss_a, rs_a, ss_y, rs_y, ss_h, rs_h, ss_s, rs_s, ss_p, rs_p):
+    p = Place()
+    s, x, y, z, h = p.s, p.x, p.y, p.z, p.h
+    sib, ypeer, hpeer = p.sibling(), p.device(y=1 - y), p.device(h=1 - h)
+    meet(p.peers())
+    t = x + 2 * z
+    local_sp = pltpu.make_async_copy(sp, SP.at[h, z, y, x, s], ls.at[0])
+    local_sp.start()
+    mine = pltpu.make_async_copy(s1.at[t], W1.at[s, h, z, y, x], ls.at[1])
+    mine.start()
+    pending = []
+    spread = []
+    for k in (1, 2, 3):
+        device, slot = p.team(k)
+        cp = remote(s1.at[slot], W1.at[s, h, z, y, x], ss_a.at[k - 1], rs_a.at[k - 1], device)
+        cp.start()
+        spread.append(cp)
+    q = 2 * h + y
+    own2 = pltpu.make_async_copy(w2, W2.at[s, q], ls.at[2])
+    own2.start()
+
+    def rows(hh, yy):
+        return W1.at[s, hh, :, yy]
+
+    def down(hh, yy):
+        return W2.at[s, 2 * hh + yy]
+
+    def push(src, dst, ss, rs, index, device):
+        cp = remote(src, dst, ss.at[index], rs.at[index], device)
+        cp.start()
+        pending.append(cp)
+        return cp
+
+    y0 = push(w2, down(h, y), ss_y, rs_y, 0, ypeer)
+    h0 = push(w2, down(h, y), ss_h, rs_h, 0, hpeer)
+    s0 = [push(w2, down(h, y), ss_s, rs_s, 0, sib)]
+    local_sp.wait()
+    views = (
+        (SP.at[h, z, y, x, s], sib),
+        (SP.at[h, z, y, x], p.team(1)[0]),
+        (SP.at[h, z, y], ypeer),
+        (SP.at[h, z], p.team(2)[0]),
+        (SP.at[h], hpeer),
+    )
+    for index, (view, device) in enumerate(views):
+        cp = remote(view, view, ss_p.at[index], rs_p.at[index], device)
+        cp.start()
+        cp.wait()
+    mine.wait()
+    for cp in spread:
+        cp.wait_recv()
+    y1 = push(rows(h, y), rows(h, y), ss_y, rs_y, 1, ypeer)
+    h1 = push(rows(h, y), rows(h, y), ss_h, rs_h, 1, hpeer)
+    s0.append(push(rows(h, y), rows(h, y), ss_s, rs_s, 1, sib))
+    g = 1 - h
+    h0.wait_recv()
+    y2 = push(down(g, y), down(g, y), ss_y, rs_y, 2, ypeer)
+    s0.append(push(down(g, y), down(g, y), ss_s, rs_s, 2, sib))
+    h1.wait_recv()
+    y3 = push(rows(g, y), rows(g, y), ss_y, rs_y, 3, ypeer)
+    s0.append(push(rows(g, y), rows(g, y), ss_s, rs_s, 3, sib))
+    v = 1 - y
+    y0.wait_recv()
+    s0.append(push(down(h, v), down(h, v), ss_s, rs_s, 4, sib))
+    y1.wait_recv()
+    s0.append(push(rows(h, v), rows(h, v), ss_s, rs_s, 5, sib))
+    y2.wait_recv()
+    s0.append(push(down(g, v), down(g, v), ss_s, rs_s, 6, sib))
+    y3.wait_recv()
+    s0.append(push(rows(g, v), rows(g, v), ss_s, rs_s, 7, sib))
+    for cp in s0:
+        cp.wait_recv()
+    own2.wait()
+    for cp in pending + spread:
+        cp.wait_send()
+
+
+def dot(a, b):
+    return jnp.dot(a, b, preferred_element_type=F32)
+
+
+def dot_nt(a, b):
+    return lax.dot_general(a, b, (((1,), (1,)), ((), ())), preferred_element_type=F32)
+
+
+def dot_tn(a, b):
+    return lax.dot_general(a, b, (((0,), (0,)), ((), ())), preferred_element_type=F32)
+
+
+def rows_norm(v):
+    centre = v - jnp.mean(v, axis=-1, keepdims=True)
+    scale = lax.rsqrt(jnp.mean(centre * centre, axis=-1, keepdims=True) + E5)
+    return centre * scale, scale
+
+
+def norm_back(cot, normed, scale, gain):
+    inner = cot * gain
+    return scale * (
+        inner
+        - jnp.mean(inner, axis=-1, keepdims=True)
+        - normed * jnp.mean(inner * normed, axis=-1, keepdims=True)
+    )
+
+
+def column_sum(v):
+    return jnp.sum(v, axis=0, keepdims=True)
+
+
+def split_heads(block, count, size):
+    lane = lax.broadcasted_iota(jnp.int32, block.shape, 1) // size
+    return jnp.concatenate([jnp.where(lane == i, block, jnp.zeros_like(block)) for i in range(count)], axis=0)
+
+
+def join_heads(block, count, size):
+    rows = block.shape[0] // count
+    lane = lax.broadcasted_iota(jnp.int32, (rows, block.shape[1]), 1) // size
+    total = jnp.where(lane == 0, block[:rows], 0.0)
+    for i in range(1, count):
+        total = jnp.where(lane == i, block[i * rows : (i + 1) * rows], total)
+    return total
+
+
+def layers_kernel(
+    x_ref, og_ref, lens, vec, bias, W1, W2,
+    lo, ig, g1, g2, sg, sb, dsum,
+    XIN, DY, A, C, FA, MIX, QKV, PR, U, HM, DZ, DAT, DU, DQ,
+    XA, XC, XF, XM, XDZ, XDAT, XDU, XDQ, RB, SB, OWN, DH,
+    ss_g, rs_g, ss_r, rs_r, ss_x, rs_x, ss_o, rs_o, ls,
+):
+    p = Place()
+    s = p.s
+    t = p.x + 2 * p.z
+    sib = p.sibling()
+    heads, hd = 4, 64
+    rows = x_ref.shape[1]
+    wide = heads * hd
+    meet((sib, p.team(1)[0], p.team(2)[0], p.team(3)[0]))
+
+    XIN[0] = x_ref[s]
+    DY[2] = og_ref[s]
+
+    def gather_start(ref, c):
+        for k in (1, 2, 3):
+            device, _ = p.team(k)
+            remote(ref.at[t], ref.at[t], ss_g.at[c, k], rs_g.at[c, k], device).start()
+
+    def gather_take(ref, c, k):
+        device, slot = p.team(k)
+        remote(ref.at[slot], ref.at[slot], ss_g.at[c, k], rs_g.at[c, k], device).wait_recv()
+
+    def gather_end(ref, c):
+        for k in (1, 2, 3):
+            device, _ = p.team(k)
+            remote(ref.at[t], ref.at[t], ss_g.at[c, k], rs_g.at[c, k], device).wait_send()
+
+    def reduce_put(c, k, part):
+        @pl.when(k == 0)
+        def _():
+            OWN[...] = part
+
+        @pl.when(k > 0)
+        def _():
+            SB[k] = part.astype(BF)
+            device, _ = p.team(k)
+            remote(SB.at[k], RB.at[c, k], ss_r.at[c, k], rs_r.at[c, k], device).start()
+
+    def reduce_end(c):
+        total = OWN[...]
+        for k in (1, 2, 3):
+            device, _ = p.team(k)
+            remote(SB.at[k], RB.at[c, k], ss_r.at[c, k], rs_r.at[c, k], device).wait()
+            total = total + RB[c, k].astype(F32)
+        return total
+
+    def each_item(ref, c, body):
+        def step(k, carry):
+            @pl.when(k > 0)
+            def _():
+                gather_take(ref, c, k)
+
+            body(k, p.team(k)[1])
+            return carry
+
+        lax.fori_loop(0, 4, step, 0)
+        gather_end(ref, c)
+
+    def share(layer, pairs):
+        @pl.when(s != layer)
+        def _():
+            for index, src, dst in pairs:
+                remote(src.at[layer], dst, ss_x.at[index], rs_x.at[index], sib).start()
+
+    def row(layer, index):
+        return vec[layer, index : index + 1, :]
+
+    def wo(layer):
+        return W2[layer, :, 0:64, :].reshape(wide, W2.shape[3])
+
+    def wdn(layer):
+        return W2[layer, :, 64:, :].reshape(W2.shape[1] * (W2.shape[2] - 64), W2.shape[3])
+
+    position = lax.broadcasted_iota(jnp.int32, (rows, 1), 0)
+    valid = (position < lens[t]).astype(F32)
+
+    def forward(layer, carry):
+        xin = XIN[layer].astype(F32)
+        normed, _ = rows_norm(xin)
+        A[layer, t] = (normed * row(layer, 0) + row(layer, 1)).astype(BF)
+        c = 2 * layer
+        gather_start(A.at[layer], c)
+
+        def attend(k, i):
+            qkv = dot(A[layer, i], W1[layer, :, : 3 * wide]).astype(BF)
+            QKV[layer, i] = qkv
+            stack = split_heads(qkv[:, :wide], heads, hd)
+            scores = dot_nt(stack, qkv[:, wide : 2 * wide]) * (hd ** (-0.5)) + bias[layer]
+            column = lax.broadcasted_iota(jnp.int32, scores.shape, 1)
+            scores = jnp.where(column < lens[i], scores, -1000000000.0)
+            raised = jnp.exp(scores - jnp.max(scores, axis=-1, keepdims=True))
+            probs = raised / jnp.sum(raised, axis=-1, keepdims=True)
+            PR[layer, i] = probs
+            mixed = join_heads(dot(probs.astype(BF), qkv[:, 2 * wide :]), heads, hd).astype(BF)
+            MIX[layer, i] = mixed
+            reduce_put(c, k, dot(mixed, wo(layer)))
+
+        each_item(A.at[layer], c, attend)
+        hmid = xin + reduce_end(c) + row(layer, 4)
+        HM[layer] = hmid
+        normed, _ = rows_norm(hmid)
+        C[layer, t] = (normed * row(layer, 2) + row(layer, 3)).astype(BF)
+        gather_start(C.at[layer], c + 1)
+
+        def feed(k, i):
+            u = dot(C[layer, i], W1[layer, :, 3 * wide :]) + row(layer, 6)
+            U[layer, i] = u
+            f = (0.5 * u * (1.0 + jnp.tanh(GELU_K * (u + 0.044715 * (u * u * u))))).astype(BF)
+            FA[layer, i] = f
+            reduce_put(c + 1, k, dot(f, wdn(layer)))
+
+        each_item(C.at[layer], c + 1, feed)
+        out = (valid * (HM[layer] + reduce_end(c + 1) + row(layer, 5))).astype(BF)
+        XIN[layer + 1] = out
+        share(layer, ((0, A, XA), (1, MIX, XM), (2, C, XC), (3, FA, XF)))
+        return carry
+
+    lax.fori_loop(0, 2, forward, 0)
+    for layer in (0, 1):
+        there = remote(XIN.at[layer + 1], lo.at[s], ss_o.at[0], rs_o.at[0], sib)
+        here = pltpu.make_async_copy(XIN.at[layer + 1], lo.at[s], ls.at[0])
+
+        @pl.when(s == layer)
+        def _():
+            here.start()
+            here.wait()
+
+        @pl.when(s != layer)
+        def _():
+            there.start()
+
+    dsum[...] = jnp.zeros_like(dsum)
+    sb[...] = jnp.zeros_like(sb)
+
+    def backward(back, carry):
+        layer = 1 - back
+        c = 4 + 2 * back
+        dyv = valid * DY[layer + 1].astype(F32)
+        DZ[layer, t] = dyv.astype(BF)
+        gather_start(DZ.at[layer], c)
+        sg[layer, 5:6, :] = column_sum(dyv)
+
+        def feed(k, i):
+            u = U[layer, i]
+            square = u * u
+            th = jnp.tanh(GELU_K * (u + 0.044715 * (square * u)))
+            slope = 0.5 * (1.0 + th) + (0.5 * GELU_K) * u * (1.0 - th * th) * (1.0 + 0.134145 * square)
+            du = (dot_nt(DZ[layer, i], wdn(layer)) * slope).astype(BF)
+            DU[layer, i] = du
+            sb[layer] += column_sum(du.astype(F32))
+            reduce_put(c, k, dot_nt(du, W1[layer, :, 3 * wide :]))
+
+        each_item(DZ.at[layer], c, feed)
+        dc = reduce_end(c)
+        normed, scale = rows_norm(HM[layer])
+        sg[layer, 2:3, :] = column_sum(dc * normed)
+        sg[layer, 3:4, :] = column_sum(dc)
+        dh = valid * DY[layer + 1].astype(F32) + norm_back(dc, normed, scale, row(layer, 2))
+        DH[...] = dh
+        dattn = dh.astype(BF)
+        DAT[layer, t] = dattn
+        gather_start(DAT.at[layer], c + 1)
+        sg[layer, 4:5, :] = column_sum(dattn.astype(F32))
+
+        def attend(k, i):
+            dmixed = dot_nt(DAT[layer, i], wo(layer)).astype(BF)
+            qkv = QKV[layer, i]
+            probs = PR[layer, i]
+            stack = split_heads(dmixed, heads, hd)
+            dprobs = dot_nt(stack, qkv[:, 2 * wide :])
+            dscores = (probs * (dprobs - jnp.sum(probs * dprobs, axis=-1, keepdims=True))).astype(BF)
+            dsum[layer] += dscores.astype(F32)
+            dq = join_heads(dot(dscores, qkv[:, wide : 2 * wide]), heads, hd) * (hd ** (-0.5))
+            dk = dot_tn(dscores, split_heads(qkv[:, :wide], heads, hd)) * (hd ** (-0.5))
+            dv = dot_tn(probs.astype(BF), stack)
+            DQ[layer, i, :, :wide] = dq.astype(BF)
+            DQ[layer, i, :, wide : 2 * wide] = dk.astype(BF)
+            DQ[layer, i, :, 2 * wide :] = dv.astype(BF)
+            reduce_put(c + 1, k, dot_nt(DQ[layer, i], W1[layer, :, : 3 * wide]))
+
+        each_item(DAT.at[layer], c + 1, attend)
+        da = reduce_end(c + 1)
+        normed, scale = rows_norm(XIN[layer].astype(F32))
+        sg[layer, 0:1, :] = column_sum(da * normed)
+        sg[layer, 1:2, :] = column_sum(da)
+        dx = DH[...] + norm_back(da, normed, scale, row(layer, 0))
+        low = dx.astype(BF)
+        DY[layer] = low
+        IGS = DH
+        IGS[...] = jnp.where(layer == 1, low.astype(F32), dx)
+        there = remote(IGS, ig.at[s], ss_o.at[1], rs_o.at[1], sib)
+        here = pltpu.make_async_copy(IGS, ig.at[s], ls.at[0])
+
+        @pl.when(s == layer)
+        def _():
+            here.start()
+            here.wait()
+
+        @pl.when(s != layer)
+        def _():
+            there.start()
+            there.wait_send()
+
+        share(layer, ((4, DZ, XDZ), (5, DAT, XDAT), (6, DU, XDU), (7, DQ, XDQ)))
+
+        @pl.when(s == layer)
+        def _():
+            for index, src, dst in (
+                (0, A, XA), (1, MIX, XM), (2, C, XC), (3, FA, XF),
+                (4, DZ, XDZ), (5, DAT, XDAT), (6, DU, XDU), (7, DQ, XDQ),
+            ):
+                remote(src.at[layer], dst, ss_x.at[index], rs_x.at[index], sib).wait_recv()
+
+            def flat(ref, lanes):
+                block = ref[:, :, lanes]
+                return block.reshape(block.shape[0] * block.shape[1], block.shape[2])
+
+            def product(own_l, other_l, own_r, other_r, lanes, span):
+                every = pl.ds(0, span)
+                return dot_tn(flat(own_l, lanes), flat(own_r, every)) + dot_tn(
+                    flat(other_l, lanes), flat(other_r, every)
+                )
+
+            def tile(j, carry):
+                lanes = pl.ds(pl.multiple_of(j * 256, 256), 256)
+                g1[lanes, : 3 * wide] = product(
+                    A.at[layer], XA, DQ.at[layer], XDQ, lanes, 3 * wide
+                ).astype(BF)
+                g1[lanes, 3 * wide :] = product(
+                    C.at[layer], XC, DU.at[layer], XDU, lanes, U.shape[3]
+                ).astype(BF)
+                g2[j, 64:, :] = product(
+                    FA.at[layer], XF, DZ.at[layer], XDZ, lanes, x_ref.shape[2]
+                ).astype(BF)
+                return carry
+
+            lax.fori_loop(0, 4, tile, 0)
+            out = product(MIX.at[layer], XM, DAT.at[layer], XDAT, pl.ds(0, wide), x_ref.shape[2]).astype(BF)
+            for j in range(4):
+                g2[j, 0:64, :] = out[j * 64 : (j + 1) * 64]
+
+        return carry
+
+    lax.fori_loop(0, 2, backward, 0)
+    for index, src, dst in (
+        (0, A, XA), (1, MIX, XM), (2, C, XC), (3, FA, XF),
+        (4, DZ, XDZ), (5, DAT, XDAT), (6, DU, XDU), (7, DQ, XDQ),
+    ):
+        remote(src.at[1 - s], dst, ss_x.at[index], rs_x.at[index], sib).wait_send()
+    remote(XIN.at[1], lo.at[1 - s], ss_o.at[0], rs_o.at[0], sib).wait()
+    remote(DH, ig.at[1 - s], ss_o.at[1], rs_o.at[1], sib).wait_recv()
+
+
+def scatter_kernel(
+    g1, g2, msg, o1, o2, so,
+    YR1, YR2, ZS1, ZS2, ZR1, ZR2, TS, TR, M, MR,
+    ss_y, rs_y, ss_h, rs_h, ss_t, rs_t, ss_m, rs_m,
+):
+    p = Place()
+    x, y, z, h, s = p.x, p.y, p.z, p.h, p.s
+    ypeer, hpeer = p.device(y=1 - y), p.device(h=1 - h)
+    meet(p.peers())
+    g, v = 1 - h, 1 - y
+    ys = []
+    for n, hh in enumerate((g, h)):
+        a = remote(g1.at[hh, :, v], YR1.at[hh], ss_y.at[2 * n], rs_y.at[2 * n], ypeer)
+        b = remote(g2.at[2 * hh + v], YR2.at[hh], ss_y.at[2 * n + 1], rs_y.at[2 * n + 1], ypeer)
+        a.start()
+        b.start()
+        ys += [a, b]
+    M[...] = msg[...]
+    steps = (
+        (M.at[g], MR.at[0:1, 0:2, 0:2, 0:2, 0:2], M.at[h], hpeer),
+    )
+    del steps
+
+    def fold(n, send, keep, land, device):
+        cp = remote(send, land, ss_m.at[n], rs_m.at[n], device)
+        cp.start()
+        cp.wait()
+        keep[...] += land[...]
+
+    fold(0, M.at[g], M.at[h], MR.at[0], hpeer)
+    fold(1, M.at[h, 1 - z], M.at[h, z], MR.at[1, 0], p.team(2)[0])
+    fold(2, M.at[h, z, v], M.at[h, z, y], MR.at[1, 1, 0], ypeer)
+    fold(3, M.at[h, z, y, 1 - x], M.at[h, z, y, x], MR.at[1, 1, 1, 0], p.team(1)[0])
+    fold(4, M.at[h, z, y, x, 1 - s], M.at[h, z, y, x, s], MR.at[1, 1, 1, 1, 0], p.sibling())
+    so[...] = M[h, z, y, x, s]
+    for cp in ys[:2]:
+        cp.wait_recv()
+    ZS1[...] = (g1[g, :, y].astype(F32) + YR1[g].astype(F32)).astype(BF)
+    ZS2[...] = (g2[2 * g + y].astype(F32) + YR2[g].astype(F32)).astype(BF)
+    za = remote(ZS1, ZR1, ss_h.at[0], rs_h.at[0], hpeer)
+    zb = remote(ZS2, ZR2, ss_h.at[1], rs_h.at[1], hpeer)
+    za.start()
+    zb.start()
+    for cp in ys[2:]:
+        cp.wait_recv()
+    za.wait_recv()
+    t = x + 2 * z
+
+    def total(zz, xx):
+        return g1[h, zz, y, xx].astype(F32) + YR1[h, zz, xx].astype(F32) + ZR1[zz, xx].astype(F32)
+
+    ts = []
+    for k in (1, 2, 3):
+        device, _ = p.team(k)
+        kx, kz = k % 2, k // 2
+        xx = x + kx * (1 - 2 * x)
+        zz = z + kz * (1 - 2 * z)
+        TS[k] = total(zz, xx).astype(BF)
+        cp = remote(TS.at[k], TR.at[k], ss_t.at[k], rs_t.at[k], device)
+        cp.start()
+        ts.append(cp)
+    o1[t] = total(z, x)
+    zb.wait_recv()
+    o2[...] = g2[2 * h + y].astype(F32) + YR2[h].astype(F32) + ZR2[...].astype(F32)
+    for k in (1, 2, 3):
+        ts[k - 1].wait_recv()
+        _, slot = p.team(k)
+        o1[slot] = TR[k].astype(F32)
+    for cp in ys + [za, zb] + ts:
+        cp.wait_send()
+
+
+def vm(n=1):
+    return [pl.BlockSpec(memory_space=pltpu.VMEM)] * n
+
+
+def hb(n=1):
+    return [pl.BlockSpec(memory_space=pltpu.HBM)] * n
+
+
+def sems(*shape):
+    return pltpu.SemaphoreType.DMA(shape)
+
+
+def shape_of(dims, kind):
+    return jax.ShapeDtypeStruct(dims, kind)
+
+
+def team_local(
+    audio_in, out_grad, item_len, rel_bucket, w_qkv, w_out, w_up, w_down,
+    ln1_gain, ln1_bias, ln2_gain, ln2_bias, b_out, b_up, b_down, rel_table,
+):
+    s = lax.axis_index("section")
+    d = lax.axis_index("dp")
+    x, y, z, h = d % 2, (d // 2) % 2, (d // 4) % 2, d // 8
+    rows, width = audio_in.shape[2], audio_in.shape[3]
+    part = w_qkv.shape[1]
+    hidden = w_up.shape[2]
+    block = hidden // 16
+    wide, team_ff = width // 4, hidden // 4
+    cols = 3 * wide + team_ff
+    tall = part + block
+
+    part_qkv = w_qkv[0].astype(BF).reshape(part, 3, 2, 2, 2, 2, 64).transpose(3, 5, 0, 1, 2, 4, 6)
+    part_up = w_up[0].astype(BF).reshape(part, 2, 2, 2, 2, block).transpose(2, 4, 0, 1, 3, 5)
+    s1 = jnp.concatenate(
+        [part_qkv.reshape(4, part, 3 * wide), part_up.reshape(4, part, team_ff)], axis=2
+    )
+    w2 = jnp.concatenate([w_out[0], w_down[0]], axis=0).astype(BF)
+    vectors = jnp.concatenate(
+        [ln1_gain, ln1_bias, ln2_gain, ln2_bias, b_out, b_down, b_up], axis=1
+    ).reshape(-1, 128)
+    vectors = lax.reduce_precision(vectors, 8, 7)
+    table = jnp.pad(lax.reduce_precision(rel_table, 8, 7), ((0, 0), (0, 96)))
+    counts = jnp.pad(item_len.astype(F32).reshape(1, 2), ((0, 0), (0, 126)))
+    small = jnp.concatenate(
+        [vectors, table, counts, jnp.zeros((8 - 2 - vectors.shape[0], 128), F32)], axis=0
+    )
+
+    W1, W2, SP = pl.pallas_call(
+        gather_kernel,
+        out_shape=(
+            shape_of((2, 2, 2, 2, 2, part, cols), BF),
+            shape_of((2, 4, tall, width), BF),
+            shape_of((2, 2, 2, 2, 2, 8, 128), F32),
+        ),
+        in_specs=hb(3),
+        out_specs=tuple(hb(3)),
+        scratch_shapes=[
+            sems(3), sems(3), sems(3), sems(4), sems(4), sems(2), sems(2), sems(8), sems(8), sems(5), sems(5),
+        ],
+        compiler_params=pltpu.CompilerParams(collective_id=0, has_side_effects=True),
+        name="gather_weights",
+    )(s1, w2, small)
+
+    SPd = SP.reshape(16, 2, 8, 128).transpose(1, 0, 2, 3)
+    six = SPd[:, :, :3].reshape(2, 16, 6, 64).transpose(0, 2, 1, 3).reshape(2, 6, width)
+    ups = SPd[:, :, 3:5].reshape(2, 2, 2, 2, 2, block)
+    ups = lax.dynamic_index_in_dim(lax.dynamic_index_in_dim(ups, z, 2, False), x, 3, False)
+    vec = jnp.concatenate([six, ups.reshape(2, 1, team_ff), jnp.zeros((2, 1, width), F32)], axis=1)
+    lens_all = SPd[0, :, 6, :2]
+    lens = lax.dynamic_index_in_dim(lens_all, s, 1, False).reshape(2, 2, 2, 2)
+    lens = lax.dynamic_index_in_dim(lax.dynamic_index_in_dim(lens, h, 0, False), y, 1, False)
+    lens = lens.reshape(4).astype(jnp.int32)
+    onehot = bucket_table(rel_bucket)
+    tables = SPd[:, :, 5, :32].reshape(2, NB, 2, 2, 2, 2)
+    tables = lax.dynamic_index_in_dim(lax.dynamic_index_in_dim(tables, z, 3, False), x, 4, False)
+    tables = tables.reshape(2, NB, 4)
+    distance = jnp.einsum("lbh,bm->lhm", tables, onehot, precision=highest).reshape(8, rows)
+    bias = toeplitz_rows(distance).reshape(2, 4, rows, rows)
+    causal = jnp.arange(rows)[None, :] <= jnp.arange(rows)[:, None]
+    bias = jnp.where(causal, bias, -1000000000.0).reshape(2, 4 * rows, rows)
+
+    W1f = W1.reshape(2, width, cols)
+    act = lambda n: pltpu.VMEM((2, 4, rows, n), BF)
+    mate = lambda n: pltpu.VMEM((4, rows, n), BF)
+    lo, ig, g1, g2, sg, sb, dsum = pl.pallas_call(
+        layers_kernel,
+        out_shape=(
+            shape_of((2, rows, width), BF),
+            shape_of((2, rows, width), F32),
+            shape_of((width, cols), BF),
+            shape_of((4, tall, width), BF),
+            shape_of((2, 8, width), F32),
+            shape_of((2, 1, team_ff), F32),
+            shape_of((2, 4 * rows, rows), F32),
+        ),
+        in_specs=vm(2) + [pl.BlockSpec(memory_space=pltpu.SMEM)] + vm(4),
+        out_specs=tuple(vm(7)),
+        scratch_shapes=[
+            pltpu.VMEM((3, rows, width), BF), pltpu.VMEM((3, rows, width), BF),
+            act(width), act(width), act(team_ff), act(wide), act(3 * wide),
+            pltpu.VMEM((2, 4, 4 * rows, rows), F32), pltpu.VMEM((2, 4, rows, team_ff), F32),
+            pltpu.VMEM((2, rows, width), F32),
+            act(width), act(width), act(team_ff), act(3 * wide),
+            mate(width), mate(width), mate(team_ff), mate(wide),
+            mate(width), mate(width), mate(team_ff), mate(3 * wide),
+            pltpu.VMEM((8, 4, rows, width), BF), pltpu.VMEM((4, rows, width), BF),
+            pltpu.VMEM((rows, width), F32), pltpu.VMEM((rows, width), F32),
+            sems(8, 4), sems(8, 4), sems(8, 4), sems(8, 4), sems(8), sems(8), sems(2), sems(2), sems(1),
+        ],
+        compiler_params=pltpu.CompilerParams(
+            collective_id=1, has_side_effects=True, vmem_limit_bytes=62 << 20
+        ),
+        name="layers",
+    )(audio_in.reshape(2, rows, width), out_grad.reshape(2, rows, width), lens, vec, bias, W1f, W2)
+
+    per_distance = diagonal_sums(dsum.reshape(8, rows, rows))
+    buckets = jnp.einsum("bm,cm->cb", onehot, per_distance, precision=highest).reshape(2, 2, 2, NB)
+    spot = ((jnp.arange(2)[:, None] == z) & (jnp.arange(2)[None, :] == x)).astype(F32)
+    table_msg = jnp.einsum("lhyb,zx->lbhzyx", buckets, spot, precision=highest).reshape(2, 16, 32)
+    table_msg = jnp.pad(table_msg, ((0, 0), (0, 0), (0, 96))).reshape(2, 16, 1, 128)
+    six_msg = sg[:, :6].reshape(2, 6, 16, 64).transpose(0, 2, 1, 3).reshape(2, 16, 3, 128)
+    up_msg = sb.reshape(2, 2, 1, 2, 1, 2, 128) * spot.reshape(1, 1, 2, 1, 2, 1, 1)
+    up_msg = up_msg.reshape(2, 16, 2, 128)
+    msg = jnp.concatenate([six_msg, up_msg, table_msg, jnp.zeros((2, 16, 2, 128), F32)], axis=2)
+    msg = msg.transpose(1, 0, 2, 3).reshape(2, 2, 2, 2, 2, 8, 128)
+
+    o1, o2, so = pl.pallas_call(
+        scatter_kernel,
+        out_shape=(
+            shape_of((4, part, cols), F32),
+            shape_of((tall, width), F32),
+            shape_of((8, 128), F32),
+        ),
+        in_specs=vm(3),
+        out_specs=tuple(vm(3)),
+        scratch_shapes=[
+            pltpu.VMEM((2, 2, 2, part, cols), BF), pltpu.VMEM((2, tall, width), BF),
+            pltpu.VMEM((2, 2, part, cols), BF), pltpu.VMEM((tall, width), BF),
+            pltpu.VMEM((2, 2, part, cols), BF), pltpu.VMEM((tall, width), BF),
+            pltpu.VMEM((4, part, cols), BF), pltpu.VMEM((4, part, cols), BF),
+            pltpu.VMEM((2, 2, 2, 2, 2, 8, 128), F32), pltpu.VMEM((2, 2, 2, 2, 2, 8, 128), F32),
+            sems(4), sems(4), sems(2), sems(2), sems(4), sems(4), sems(5), sems(5),
+        ],
+        compiler_params=pltpu.CompilerParams(
+            collective_id=2, has_side_effects=True, vmem_limit_bytes=62 << 20
+        ),
+        name="scatter_grads",
+    )(g1.reshape(2, 2, 2, 2, part, cols), g2, msg)
+
+    grad_qkv = o1[:, :, : 3 * wide].reshape(2, 2, part, 3, 2, 2, 64).transpose(2, 3, 4, 0, 5, 1, 6)
+    grad_up = o1[:, :, 3 * wide :].reshape(2, 2, part, 2, 2, block).transpose(2, 3, 0, 4, 1, 5)
+    six_out = so[:3].reshape(6, 64)
+    return (
+        lo[None, :, None],
+        ig[None, :, None],
+        grad_qkv.reshape(1, part, 3 * width),
+        o2[None, :part],
+        grad_up.reshape(1, part, hidden),
+        o2[None, part:],
+        six_out[0:1],
+        six_out[1:2],
+        six_out[2:3],
+        six_out[3:4],
+        six_out[4:5],
+        so[3:5].reshape(1, block),
+        six_out[5:6],
+        so[5:6, :32],
+    )
+
+
 def solution(mesh):
+    fits = mesh.shape["dp"] == 16 and mesh.shape["section"] == 2
     return jax.shard_map(
-        local,
+        team_local if fits else local,
         mesh=mesh,
         in_specs=(
             P(None, "dp", None, None),

time: 1680 us -> 481 us (0.29)
  waiting for transfers between devices: 1190 us -> 0 us
  Pallas kernels: 0 us -> 444 us
  blocking collectives: 189 us -> 0 us
  matrix products: 148 us -> 0.25 us
  other arithmetic: 52.8 us -> 7.22 us
  local copies, waits for them, and re-layouts: 51.4 us -> 27.4 us
  between operations: 18.5 us -> 1.15 us
    reduce_scatter x4 -> x0, waiting for transfers between devices: 884 us -> none  [the longest x1 355 us: local(): lax.psum_scatter(totals[3], 'dp', scatter_dimension=0, tiled=True)]
    pallas_call x0 -> x3, Pallas kernels: none -> 444 us  [the longest x1 191 us: team_local(): pl.pallas_call(layers_kernel, out_shape=(shape_of((2, rows, width), BF),...]
    all_gather x4 -> x0, waiting for transfers between devices: 263 us -> none  [the longest x1 114 us: local(): lax.all_gather(up_part, 'dp', axis=0, tiled=True)]
    dot_general x43 -> x2, matrix products: 148 us -> 0.25 us  [the longest x1 0.13 us: team_local(): jnp.einsum('lbh,bm->lhm', tables, onehot, precision=highest)]
    all_gather x2 -> x0, blocking collectives: 115 us -> none  [the longest x1 79 us: local(): lax.all_gather(gain_one_part, 'dp', axis=0, tiled=True)]
    unnamed x1 -> x0, blocking collectives: 74.5 us -> none
    ppermute x4 -> x0, waiting for transfers between devices: 43.4 us -> none  [passed_along(): return lax.ppermute(block, axis, route)]
  transfers between devices with their start and end apart: 12 -> 0, of which waited for: 10 -> 0; matrix products, arithmetic and copies ran while one was open for 4% -> 0% of each run, Pallas kernels for 0% -> 0%
where the time goes in v1:
time: 481 us; the launch traced here: 480 us
  Pallas kernels  444 us (92%)
  local copies, waits for them, and re-layouts  27.4 us (6%)
  other arithmetic  7.22 us (2%)
    pallas_call x1, Pallas kernels, team_local(): pl.pallas_call(layers_kernel, out_shape=(shape_of((2, rows, width), BF),...  191 us
    pallas_call x1, Pallas kernels, team_local(): pl.pallas_call(scatter_kernel, out_shape=(shape_of((4, part, cols), F32),...  152 us
    pallas_call x1, Pallas kernels, team_local(): pl.pallas_call(gather_kernel, out_shape=(shape_of((2, 2, 2, 2, 2, part, c...  101 us

profile of v1, /device:TPU:0, one launch (start us, length us, event | category | flops | bytes accessed | tf_op | source)
XLA Modules:
  0.0 480.2 jit_solution(3962519985160675725)
XLA Ops:
  0.8 0.9 concatenate.30
  1.7 0.7 convert_bitcast_fusion.2
  2.3 0.7 reduce_precision.11
  3.0 0.7 fusion.4.sp
  3.6 1.2 convert_element_type.37
  4.8 0.5 convert_element_type.38
  5.3 0.4 copy.76
  5.7 0.5 reshape.201
  6.3 0.4 convert_element_type.40
  6.7 0.4 copy.77
  7.1 0.4 reshape.202
  7.5 1.0 pad_maximum_fusion.s1
  8.6 0.9 pad_maximum_fusion.1.w2
  9.4 101.2 %gather_weights.1 = (bf16[2,2,2,2,2,64,1792]{6,5,4,3,2,1,0:T(8,128)(2,1)}, bf16[2,4,320,1024]{3,2,1,0:T(8,128)(2,1)}, f32[2,2,2,2,2,8,128]{6,5,4,3,2,1,0:T(8,128)}) custom-call(bf16[4,64,1792]{2,1,0:T(8,128)(2,1)} %pad_maximum_fusion.s1, bf16[320,1024]{1,0:T(8,128)(2,1)} %pad_maximum_fusion.1.w2, f32[8,128]{1,0:T(8,128)} %fusion.4.sp), custom_call_target="tpu_custom_call" | custom-call | tf_op jit(solution)/shard_map/gather_weights/pallas_call | solution.py:986
  110.7 0.9 copy.78
  111.6 0.4 reshape_squeeze.3
  112.1 0.2 constant_dynamic-slice_fusion
  112.4 0.1 fusion.1
  112.7 0.3 tile.10
  113.0 0.9 reshape.211
  113.9 0.2 slice.89
  114.2 0.8 bitcast_select_fusion.bias
  115.3 0.7 maximum_maximum_fusion.vec
  116.0 0.2 dynamic-slice_reduce_fusion
  116.3 0.6 convert_element_type.43.lens
  116.9 191.1 %layers.1 = (bf16[2,96,1024]{2,1,0:T(8,128)(2,1)}, f32[2,96,1024]{2,1,0:T(8,128)}, bf16[1024,1792]{1,0:T(8,128)(2,1)}, bf16[4,320,1024]{2,1,0:T(8,128)(2,1)}, f3...) custom-call(bf16[2,96,1024]{2,1,0:T(8,128)(2,1)} %bitcast.85, bf16[2,96,1024]{2,1,0:T(8,128)(2,1)} %bitcast.86, ...), custom_call_target="tpu_custom_call" | custom-call | tf_op jit(solution)/shard_map/layers/pallas_call | solution.py:1023
  308.1 1.3 concatenate.34
  309.3 0.4 reshape.218
  309.8 0.3 reshape.219
  310.7 0.2 multiply_bitcast_fusion
  310.9 0.4 reshape.221
  312.0 0.7 copy.66
  312.6 151.8 %scatter_grads.1 = (f32[4,64,1792]{2,1,0:T(8,128)}, f32[320,1024]{1,0:T(8,128)}, f32[8,128]{1,0:T(8,128)}) custom-call(bf16[2,2,2,2,64,1792]{5,4,3,2,1,0:T(8,128)(2,1)} %bitcast.73, bf16[4,320,1024]{2,1,0:T(8,128)(2,1)} %get-tuple-element.33.g2, f32[2,2,2,2,2,8,128]{6,5,4,3,2,1,0:T(8,128)} %bitcast.79), custom_call_target="tpu_custom_call" | custom-call | tf_op jit(solution)/shard_map/scatter_grads/pallas_call | solution.py:1065
  464.4 1.2 slice.71
  465.6 1.0 reshape.224
  466.7 1.2 copy.67
  467.9 2.3 reshape.225
  470.2 1.3 slice.73
  471.5 0.9 reshape.226
  472.4 0.8 copy.68
  473.2 1.8 reshape.227
  475.1 1.0 slice_bitcast_fusion
  476.1 0.7 slice_bitcast_fusion.1
  476.9 0.5 fusion.7
  477.5 0.6 slice.81
  478.0 0.5 slice.83
  478.5 0.7 copy.81
  479.3 0.9 copy.82
  (66 shorter events, 2.3 us)
Async XLA Ops:
  4.8 1.4 copy-start.1
  6.7 1.8 copy-start.2
  7.4 1.1 copy-start.5
  8.6 103.8 %copy-start.9 = (s32[96]{0:T(128)S(1)}, s32[96]{0:T(128)}, u32[]{:S(2)}) copy-start(s32[96]{0:T(128)} %param.19) | copy-start | bytes 1156
  309.8 1.5 copy-start.7
  309.8 1.7 copy-start.6
  472.4 2.6 copy-start
  475.1 1.8 copy-start.8
  475.1 3.5 copy-start.4
  475.1 4.2 copy-start.3

commit v2 on v0

--- a/solution.py
+++ b/solution.py
@@ -1,6 +1,8 @@
 import jax
 import jax.numpy as jnp
 from jax import lax
+from jax.experimental import pallas as pl
+from jax.experimental.pallas import tpu as pltpu
 from jax.sharding import PartitionSpec as P
 
 H = 16
@@ -424,9 +426,940 @@
     return (outputs[None, :, None], input_grads[None, :, None]) + grads_out
 
 
+E5 = 1e-05
+F32 = jnp.float32
+BF = jnp.bfloat16
+MESH = pl.DeviceIdType.MESH
+GELU_K = 0.7978845608028654
+HD = 64
+
+
+class Place:
+    def __init__(self):
+        self.s = lax.axis_index("section")
+        d = lax.axis_index("dp")
+        self.x = d % 2
+        self.y = (d // 2) % 2
+        self.z = (d // 4) % 2
+        self.h = d // 8
+        self.t = self.x + 2 * self.z
+
+    def device(self, s=None, x=None, y=None, z=None, h=None):
+        s = self.s if s is None else s
+        x = self.x if x is None else x
+        y = self.y if y is None else y
+        z = self.z if z is None else z
+        h = self.h if h is None else h
+        return (s, x + 2 * y + 4 * z + 8 * h)
+
+    def sibling(self):
+        return self.device(s=1 - self.s)
+
+    def across_y(self):
+        return self.device(y=1 - self.y)
+
+    def across_h(self):
+        return self.device(h=1 - self.h)
+
+    def mate(self, k):
+        return self.x + (k % 2) * (1 - 2 * self.x), self.z + (k // 2) * (1 - 2 * self.z)
+
+    def team(self, k):
+        px, pz = self.mate(k)
+        return self.device(x=px, z=pz), px + 2 * pz
+
+
+def remote(src, dst, send, recv, device):
+    return pltpu.make_async_remote_copy(
+        src_ref=src, dst_ref=dst, send_sem=send, recv_sem=recv, device_id=device, device_id_type=MESH
+    )
+
+
+def dot(a, b):
+    return jnp.dot(a, b, preferred_element_type=F32)
+
+
+def dot_nt(a, b):
+    return lax.dot_general(a, b, (((1,), (1,)), ((), ())), preferred_element_type=F32)
+
+
+def dot_tn(a, b):
+    return lax.dot_general(a, b, (((0,), (0,)), ((), ())), preferred_element_type=F32)
+
+
+def rows_norm(v):
+    centre = v - jnp.mean(v, axis=-1, keepdims=True)
+    scale = lax.rsqrt(jnp.mean(centre * centre, axis=-1, keepdims=True) + E5)
+    return centre * scale, scale
+
+
+def norm_back(cot, normed, scale, gain):
+    inner = cot * gain
+    return scale * (
+        inner
+        - jnp.mean(inner, axis=-1, keepdims=True)
+        - normed * jnp.mean(inner * normed, axis=-1, keepdims=True)
+    )
+
+
+def column_sum(v):
+    return jnp.sum(v, axis=0, keepdims=True)
+
+
+def lanes_of(shape, axis=1):
+    return lax.broadcasted_iota(jnp.int32, shape, axis)
+
+
+def split_heads(block, count, size):
+    lane = lanes_of(block.shape) // size
+    return jnp.concatenate([jnp.where(lane == i, block, jnp.zeros_like(block)) for i in range(count)], axis=0)
+
+
+def join_heads(block, count, size):
+    rows = block.shape[0] // count
+    lane = lanes_of((rows, block.shape[1])) // size
+    total = jnp.where(lane == 0, block[:rows], 0.0)
+    for i in range(1, count):
+        total = jnp.where(lane == i, block[i * rows : (i + 1) * rows], total)
+    return total
+
+
+def turn(block, shift):
+    width = block.shape[1]
+    shift = shift % width
+    return jnp.concatenate([block[:, width - shift :], block[:, : width - shift]], axis=1)
+
+
+def skew(block, length, sign):
+    row = lanes_of(block.shape, 0) % length
+    for bit in range(7):
+        block = jnp.where((row // 2**bit) % 2 == 1, turn(block, sign * 2**bit), block)
+    return block
+
+
+class Part:
+    def __init__(self, index, pieces, **refs):
+        self.index = index
+        self.pieces = pieces
+        self.chunks = 2 + pieces
+        for name, ref in refs.items():
+            setattr(self, name, ref)
+
+    def strip(self, c, rows):
+        step = rows // self.pieces
+        return pl.ds((c - 2) * step, step)
+
+
+def step_kernel(
+    x_ref, og_ref, il_ref, rb_ref, wq_in, wo_in, wu_in, wd_in,
+    v0_ref, v1_ref, v2_ref, v3_ref, v4_ref, v5_ref, bu_ref, rt_ref,
+    lo, ig, OQ, OO, OU, OD, OT,
+    SQ, SU, WQ, WO, WU, WD, XIN, DY, A, C, FA, MIX, QKV, PR, UF, HM, DZ, DAT, DU, DQ,
+    XA, XC, XF, XM, XDZ, XDAT, XDU, XDQ, RB, SB, OWN, DH,
+    GQ, GO, GU, GD, YQ, YO, YU, YD, ZSQ, ZSO, ZSU, ZSD, ZRQ, ZRO, ZRU, ZRD, TSQ, TRQ, TSU, TRU,
+    SPT, SPX, VEC, LEN, BIAS, PD, SGV, SBU, DS, MT, MR,
+    ls, ss_a, rs_a, ss_wy, rs_wy, ss_wh, rs_wh, ss_ws, rs_ws, ss_p, rs_p,
+    ss_g, rs_g, ss_r, rs_r, ss_x, rs_x, ss_o, rs_o,
+    ss_gy, rs_gy, ss_gh, rs_gh, ss_gt, rs_gt, ss_m, rs_m,
+):
+    p = Place()
+    s, x, y, z, h, t = p.s, p.x, p.y, p.z, p.h, p.t
+    sib, ypeer, hpeer = p.sibling(), p.across_y(), p.across_h()
+    rows, width = x_ref.shape[1], x_ref.shape[2]
+    heads = 4
+    wide = heads * HD
+    ff = FA.shape[3]
+    part_rows = WO.shape[2]
+    block = WD.shape[2]
+
+    first = Part(0, 1, W=WQ, V=WO, S=SQ, G=GQ, R=GO, Y=YQ, YR=YO, ZS=ZSQ, ZSR=ZSO, ZR=ZRQ, ZRR=ZRO,
+                 TS=TSQ, TR=TRQ, O=OQ, OR=OO)
+    second = Part(1, 2, W=WU, V=WD, S=SU, G=GU, R=GD, Y=YU, YR=YD, ZS=ZSU, ZSR=ZSD, ZR=ZRU, ZRR=ZRD,
+                  TS=TSU, TR=TRU, O=OU, OR=OD)
+
+    loads = [
+        pltpu.make_async_copy(wq_in.at[:, pl.ds(width * i, width)], UF.at[pl.ds(576 + 64 * i, 64)], ls.at[i])
+        for i in range(3)
+    ]
+    loads.append(pltpu.make_async_copy(wo_in, UF.at[pl.ds(0, 64)], ls.at[3]))
+    loads += [
+        pltpu.make_async_copy(wu_in.at[:, pl.ds(width * i, width)], UF.at[pl.ds(320 + 64 * i, 64)], ls.at[4 + i])
+        for i in range(4)
+    ]
+    loads.append(pltpu.make_async_copy(wd_in, UF.at[pl.ds(64, 256)], ls.at[8]))
+    for cp in loads:
+        cp.start()
+
+    bell = pltpu.get_barrier_semaphore()
+    everyone = (sib, p.team(1)[0], p.team(2)[0], p.team(3)[0], ypeer, hpeer)
+    for peer in everyone:
+        pl.semaphore_signal(bell, inc=1, device_id=peer, device_id_type=MESH)
+
+    for cp in loads[:4]:
+        cp.wait()
+    for i in range(3):
+        for hh in range(2):
+            for zz in range(2):
+                base = (2 * zz + 4 * hh) * 128
+                even = UF[576 + 64 * i : 640 + 64 * i, base : base + 128].astype(BF)
+                odd = UF[576 + 64 * i : 640 + 64 * i, base + 128 : base + 256].astype(BF)
+                at = (2 * i + hh) * 128
+                SQ[2 * zz, :, at : at + 128] = jnp.concatenate([even[:, :HD], odd[:, :HD]], axis=1)
+                SQ[2 * zz + 1, :, at : at + 128] = jnp.concatenate([even[:, HD:], odd[:, HD:]], axis=1)
+    WQ[s, h, z, y, x] = SQ[t]
+    q = 2 * h + y
+    WO[s, q] = UF[0:64, :].astype(BF)
+    pl.semaphore_wait(bell, len(everyone))
+
+    def w_team(part, k):
+        device, slot = p.team(k)
+        return remote(
+            part.S.at[slot], part.W.at[s, h, z, y, x], ss_a.at[part.index, k], rs_a.at[part.index, k], device
+        )
+
+    def w_view(part, c, hh, yy):
+        if c < 2:
+            return part.W.at[s, hh, c, yy]
+        return part.V.at[s, 2 * hh + yy, part.strip(c, part.V.shape[2])]
+
+    def w_y(part, c, n):
+        view = w_view(part, c, h + n * (1 - 2 * h), y)
+        return remote(view, view, ss_wy.at[part.index, n, c], rs_wy.at[part.index, n, c], ypeer)
+
+    def w_h(part, c):
+        view = w_view(part, c, h, y)
+        return remote(view, view, ss_wh.at[part.index, c], rs_wh.at[part.index, c], hpeer)
+
+    def w_s(part, c, hh, yy):
+        view = w_view(part, c, hh, yy)
+        n = 2 * hh + yy
+        return remote(view, view, ss_ws.at[part.index, n, c], rs_ws.at[part.index, n, c], sib)
+
+    def w_spread(part):
+        for k in (1, 2, 3):
+            w_team(part, k).wait_recv()
+        for c in range(part.chunks):
+            w_h(part, c).start()
+            w_y(part, c, 0).start()
+            w_s(part, c, h, y).start()
+
+    def w_pass(part, c):
+        w_h(part, c).wait_recv()
+        w_y(part, c, 1).start()
+        w_s(part, c, 1 - h, y).start()
+
+    def w_last(part):
+        for c in range(part.chunks):
+            w_y(part, c, 0).wait_recv()
+            w_s(part, c, h, 1 - y).start()
+        for c in range(part.chunks):
+            w_y(part, c, 1).wait_recv()
+            w_s(part, c, 1 - h, 1 - y).start()
+
+    def w_other(part):
+        for c in range(part.chunks):
+            for n in range(4):
+                w_s(part, c, n // 2, n % 2).wait_recv()
+
+    for k in (1, 2, 3):
+        w_team(first, k).start()
+    for cp in loads[4:]:
+        cp.wait()
+    for hh in range(2):
+        for zz in range(2):
+            for yy in range(2):
+                for xx in range(2):
+                    at = (2 * hh + yy) * block
+                    low = 320 + 64 * (zz + 2 * hh)
+                    col = (xx + 2 * yy) * block
+                    SU[xx + 2 * zz, :, at : at + block] = UF[low : low + 64, col : col + block].astype(BF)
+    WU[s, h, z, y, x] = SU[t]
+    WD[s, q] = UF[64 : 64 + block, :].astype(BF)
+    for k in (1, 2, 3):
+        w_team(second, k).start()
+
+    @pl.when(s == 0)
+    def _():
+        w_spread(first)
+
+    lane = lanes_of((1, 128))
+    zero = jnp.zeros((1, 128), F32)
+    pair = [jnp.concatenate([v[...], v[...]], axis=1) for v in (v0_ref, v1_ref, v2_ref, v3_ref, v4_ref, v5_ref)]
+    lines = [jnp.where(lane // HD == x, v, zero) for v in pair]
+    for xx in range(2):
+        for i in range(2):
+            lines.append(jnp.where(x == xx, bu_ref[:, 128 * i : 128 * i + 128], zero))
+    table = jnp.concatenate([rt_ref[...], jnp.zeros((1, 96), F32)], axis=1)
+    counts = jnp.where(lane == 0, il_ref[0:1, :].astype(F32), jnp.where(lane == 1, il_ref[1:2, :].astype(F32), zero))
+    for piece in (table, counts):
+        for xx in range(2):
+            lines.append(jnp.where(x == xx, piece, zero))
+    for i in range(2):
+        lines.append(zero)
+    for i in range(16):
+        SPX[0, i : i + 1, :] = lines[i].astype(BF).astype(F32)
+
+    def swap(n, src, dst, device):
+        cp = remote(src, dst, ss_p.at[n], rs_p.at[n], device)
+        cp.start()
+        cp.wait()
+
+    swap(0, SPX.at[0], SPX.at[1], p.team(1)[0])
+    SPT[h, z, y, s] = SPX[0] + SPX[1]
+    for n, (view, device) in enumerate(
+        (
+            (SPT.at[h, z, y, s], sib),
+            (SPT.at[h, z, y], ypeer),
+            (SPT.at[h, z], p.team(2)[0]),
+            (SPT.at[h], hpeer),
+        )
+    ):
+        swap(n + 1, view, view, device)
+
+    for hh in range(2):
+        for zz in range(2):
+            for yy in range(2):
+                at = (yy + 2 * zz + 4 * hh) * 128
+                for i in range(2):
+                    VEC[i, 0:6, at : at + 128] = SPT[hh, zz, yy, i, 0:6, :]
+    for i in range(2):
+        for hh in range(2):
+            for yy in range(2):
+                tile = SPT[hh, z, yy, i]
+                for r in range(2):
+                    at = (2 * hh + yy) * block + 128 * r
+                    VEC[i, 6:7, at : at + 128] = jnp.where(x == 0, tile[6 + r : 7 + r], tile[8 + r : 9 + r])
+    for zz in range(2):
+        tile = SPT[h, zz, y, 0]
+        for xx in range(2):
+            count = jnp.sum(jnp.where(lane == s, tile[12 + xx : 13 + xx], 0.0), axis=1, keepdims=True)
+            LEN[xx + 2 * zz] = jnp.broadcast_to(count, (8, 128))
+
+    mark = jnp.concatenate([rb_ref[...], jnp.full((1, 128 - rows), 2 * NB, jnp.int32)], axis=1).astype(BF)
+    mark = jnp.broadcast_to(mark, (8, 128))
+    flip = ((lanes_of((128, 128), 0) + lanes_of((128, 128))) % 128 == 0).astype(F32).astype(BF)
+    mark = dot(mark, flip)[0:1]
+    onehot = (lanes_of((NB, 128), 0).astype(F32) == mark).astype(F32)
+    for i in range(2):
+        lines = []
+        for hh in range(2):
+            for zz in range(2):
+                for yy in range(2):
+                    tile = SPT[hh, zz, yy, i]
+                    for xx in range(2):
+                        for b in range(2):
+                            lines.append(tile[10 + xx : 11 + xx, 16 * b : 16 * b + 16])
+        by_bucket = jnp.concatenate([jnp.concatenate(lines, axis=0), jnp.zeros((NB, 112), F32)], axis=1)
+        PD[...] = dot_tn(by_bucket.astype(BF), onehot.astype(BF))
+        stack = []
+        for hh in range(2):
+            for yy in range(2):
+                line = PD[pl.ds(x + 2 * yy + 4 * z + 8 * hh, 1), :]
+                stack.append(jnp.broadcast_to(line, (rows, 128)))
+        grid = skew(jnp.concatenate(stack, axis=0), rows, 1)[:, :rows]
+        causal = lanes_of(grid.shape) <= lanes_of(grid.shape, 0) % rows
+        BIAS[i] = jnp.where(causal, grid, -1000000000.0)
+
+    def gather_copy(ref, c, k):
+        return remote(ref.at[t], ref.at[t], ss_g.at[c, k], rs_g.at[c, k], p.team(k)[0])
+
+    def gather_start(ref, c):
+        gather_copy(ref, c, 1).start()
+        gather_copy(ref, c, 2).start()
+
+    def gather_take(ref, c, k):
+        device, slot = p.team(k)
+        remote(ref.at[slot], ref.at[slot], ss_g.at[c, k], rs_g.at[c, k], device).wait_recv()
+
+    def reduce_copy(c, k):
+        return remote(SB.at[k], RB.at[k], ss_r.at[c, k], rs_r.at[c, k], p.team(k)[0])
+
+    def reduce_put(c, k, value):
+        @pl.when(k == 0)
+        def _():
+            OWN[...] = value
+
+        @pl.when(k > 0)
+        def _():
+            SB[k] = value.astype(BF)
+            reduce_copy(c, k).start()
+
+    def reduce_end(c):
+        total = OWN[...]
+        for k in (1, 2, 3):
+            reduce_copy(c, k).wait()
+            total = total + RB[k].astype(F32)
+        return total
+
+    def each_item(ref, c, body, aside):
+        def step(k, carry):
+            @pl.when(k > 0)
+            def _():
+                gather_take(ref, c, k)
+
+            body(k, p.team(k)[1])
+
+            @pl.when(k == 0)
+            def _():
+                gather_copy(ref, c, 3).start()
+
+            aside(k)
+            return carry
+
+        lax.fori_loop(0, 4, step, 0)
+        for k in (1, 2, 3):
+            gather_copy(ref, c, k).wait_send()
+
+    def at_step(k, here, n, what):
+        @pl.when(jnp.logical_and(here, k == n))
+        def _():
+            what()
+
+    pairs = ((A, XA), (MIX, XM), (C, XC), (FA, XF), (DZ, XDZ), (DAT, XDAT), (DU, XDU), (DQ, XDQ))
+
+    def share_copy(i, layer):
+        return remote(pairs[i][0].at[layer], pairs[i][1], ss_x.at[i], rs_x.at[i], sib)
+
+    def share(layer, which):
+        @pl.when(s != layer)
+        def _():
+            for i in which:
+                share_copy(i, layer).start()
+
+    def row(layer, index):
+        return VEC[layer, index : index + 1, :]
+
+    def w_qkv(layer):
+        return WQ[layer].reshape(width, 3 * wide)
+
+    def w_up(layer):
+        return WU[layer].reshape(width, ff)
+
+    def w_out(layer):
+        return WO[layer].reshape(wide, width)
+
+    def w_down(layer):
+        return WD[layer].reshape(ff, width)
+
+    def u_rows(layer, i):
+        return pl.ds(pl.multiple_of((layer * 4 + i) * rows, 8), rows)
+
+    position = lanes_of((rows, 1), 0).astype(F32)
+    valid = (position < LEN[t][0:1, 0:1]).astype(F32)
+
+    def g_own(part, c, hh, yy):
+        if c < 2:
+            return part.G.at[hh, c, yy]
+        return part.R.at[2 * hh + yy, part.strip(c, part.R.shape[1])]
+
+    def g_land(part, c, n):
+        if c < 2:
+            return part.Y.at[n, c]
+        return part.YR.at[n, part.strip(c, part.R.shape[1])]
+
+    def g_half(n):
+        return (1 - h) + n * (2 * h - 1)
+
+    def g_y(part, c, n):
+        return remote(
+            g_own(part, c, g_half(n), 1 - y), g_land(part, c, n),
+            ss_gy.at[part.index, n, c], rs_gy.at[part.index, n, c], ypeer,
+        )
+
+    def g_z(part, c, out):
+        if c < 2:
+            return (part.ZS if out else part.ZR).at[c]
+        return (part.ZSR if out else part.ZRR).at[part.strip(c, part.R.shape[1])]
+
+    def g_h(part, c):
+        return remote(
+            g_z(part, c, True), g_z(part, c, False), ss_gh.at[part.index, c], rs_gh.at[part.index, c], hpeer
+        )
+
+    def g_t(part, k):
+        return remote(
+            part.TS.at[k], part.TR.at[k], ss_gt.at[part.index, k], rs_gt.at[part.index, k], p.team(k)[0]
+        )
+
+    def flat(ref, span):
+        value = ref[:, :, span]
+        return value.reshape(value.shape[0] * value.shape[1], value.shape[2])
+
+    def product(left, right, span):
+        every = pl.ds(0, right[0].shape[2])
+        return dot_tn(flat(left[0], span), flat(right[0], every)) + dot_tn(
+            flat(left[1], span), flat(right[1], every)
+        )
+
+    def g_make(part):
+        if part is first:
+            need = (0, 1, 5, 7)
+            big_l, big_r = (A.at[s], XA), (DQ.at[s], XDQ)
+            small_l, small_r = (MIX.at[s], XM), (DAT.at[s], XDAT)
+            small_span = HD
+        else:
+            need = (2, 3, 4, 6)
+            big_l, big_r = (C.at[s], XC), (DU.at[s], XDU)
+            small_l, small_r = (FA.at[s], XF), (DZ.at[s], XDZ)
+            small_span = block
+        for i in need:
+            share_copy(i, s).wait_recv()
+        if part is first:
+            value = product(small_l, small_r, pl.ds(0, wide)).astype(BF)
+            for i in range(4):
+                part.R[i] = value[i * small_span : (i + 1) * small_span]
+
+        def tile(n, carry):
+            hh = g_half(n)
+            for zz in range(2):
+                span = pl.ds(pl.multiple_of((2 * hh + zz) * 256, 256), 256)
+                value = product(big_l, big_r, span).astype(BF)
+                part.G[hh, zz] = value.reshape(2, 2, part_rows, value.shape[1])
+                g_y(part, zz, n).start()
+            if part is second:
+                for yy in (1 - y, y):
+                    span = pl.ds(pl.multiple_of((2 * hh + yy) * 256, 256), 256)
+                    part.R[2 * hh + yy] = product(small_l, small_r, span).astype(BF)
+                    if yy is not y:
+                        for c in range(2, part.chunks):
+                            g_y(part, c, n).start()
+            else:
+                g_y(part, 2, n).start()
+            return carry
+
+        lax.fori_loop(0, 2, tile, 0)
+
+    def g_fold(part, c):
+        g_y(part, c, 0).wait_recv()
+        g_z(part, c, True)[...] = (
+            g_own(part, c, 1 - h, y)[...].astype(F32) + g_land(part, c, 0)[...].astype(F32)
+        ).astype(BF)
+        g_h(part, c).start()
+
+    def g_total(part):
+        for c in range(part.chunks):
+            g_y(part, c, 1).wait_recv()
+            g_h(part, c).wait_recv()
+
+        def total(xx, zz):
+            return (
+                part.G[h, zz, y, xx].astype(F32) + part.Y[1, zz, xx].astype(F32) + part.ZR[zz, xx].astype(F32)
+            )
+
+        for k in (1, 2, 3):
+            part.TS[k] = total(*p.mate(k)).astype(BF)
+            g_t(part, k).start()
+        part.O[t] = total(x, z)
+        part.OR[...] = part.R[q].astype(F32) + part.YR[1].astype(F32) + part.ZRR[...].astype(F32)
+
+    def g_end(part):
+        for k in (1, 2, 3):
+            g_t(part, k).wait_recv()
+            part.O[p.team(k)[1]] = part.TR[k].astype(F32)
+
+    XIN[0] = x_ref[s]
+    DY[2] = og_ref[s]
+
+    @pl.when(s == 0)
+    def _():
+        for c in range(first.chunks):
+            w_pass(first, c)
+        w_spread(second)
+
+    def forward(layer, carry):
+        mine = s == layer
+        coming = jnp.logical_and(s == 1, layer == 0)
+        xin = XIN[layer].astype(F32)
+        normed, _ = rows_norm(xin)
+        A[layer, t] = (normed * row(layer, 0) + row(layer, 1)).astype(BF)
+        c = 2 * layer
+        gather_start(A.at[layer], c)
+
+        @pl.when(mine)
+        def _():
+            w_last(first)
+
+        @pl.when(s != layer)
+        def _():
+            w_other(first)
+
+        def attend(k, i):
+            qkv = dot(A[layer, i], w_qkv(layer)).astype(BF)
+            QKV[layer, i] = qkv
+            stack = split_heads(qkv[:, :wide], heads, HD)
+            scores = dot_nt(stack, qkv[:, wide : 2 * wide]) * (HD ** (-0.5)) + BIAS[layer]
+            column = lanes_of(scores.shape).astype(F32)
+            scores = jnp.where(column < LEN[i][0:1, 0:1], scores, -1000000000.0)
+            raised = jnp.exp(scores - jnp.max(scores, axis=-1, keepdims=True))
+            probs = raised / jnp.sum(raised, axis=-1, keepdims=True)
+            PR[layer, i] = probs
+            mixed = join_heads(dot(probs.astype(BF), qkv[:, 2 * wide :]), heads, HD).astype(BF)
+            MIX[layer, i] = mixed
+            reduce_put(c, k, dot(mixed, w_out(layer)))
+
+        def pass_on(k):
+            for n in range(3):
+                at_step(k, mine, n + 1, lambda n=n: w_pass(second, n))
+
+        each_item(A.at[layer], c, attend, pass_on)
+        share(layer, (0, 1))
+        hmid = xin + reduce_end(c) + row(layer, 4)
+        HM[layer] = hmid
+        normed, _ = rows_norm(hmid)
+        C[layer, t] = (normed * row(layer, 2) + row(layer, 3)).astype(BF)
+        gather_start(C.at[layer], c + 1)
+
+        @pl.when(mine)
+        def _():
+            w_pass(second, 3)
+            w_last(second)
+
+        @pl.when(s != layer)
+        def _():
+            w_other(second)
+
+        def feed(k, i):
+            u = dot(C[layer, i], w_up(layer)) + row(layer, 6)
+            UF[u_rows(layer, i), :] = u
+            f = (0.5 * u * (1.0 + jnp.tanh(GELU_K * (u + 0.044715 * (u * u * u))))).astype(BF)
+            FA[layer, i] = f
+            reduce_put(c + 1, k, dot(f, w_down(layer)))
+
+        def prepare(k):
+            at_step(k, coming, 0, lambda: w_spread(first))
+            for n in range(3):
+                at_step(k, coming, n + 1, lambda n=n: w_pass(first, n))
+            at_step(k, coming, 3, lambda: w_spread(second))
+
+        each_item(C.at[layer], c + 1, feed, prepare)
+        share(layer, (2, 3))
+        out = (valid * (HM[layer] + reduce_end(c + 1) + row(layer, 5))).astype(BF)
+        XIN[layer + 1] = out
+        return carry
+
+    lax.fori_loop(0, 2, forward, 0)
+    for layer in (0, 1):
+
+        @pl.when(s == layer)
+        def _(layer=layer):
+            lo[s] = XIN[layer + 1]
+
+        @pl.when(s != layer)
+        def _(layer=layer):
+            remote(XIN.at[layer + 1], lo.at[s], ss_o.at[0], rs_o.at[0], sib).start()
+
+    DS[...] = jnp.zeros_like(DS)
+    SBU[...] = jnp.zeros_like(SBU)
+    SGV[...] = jnp.zeros_like(SGV)
+
+    def backward(back, carry):
+        layer = 1 - back
+        mine = s == layer
+        done = jnp.logical_and(s == 1, layer == 0)
+        c = 4 + 2 * back
+        dyv = valid * DY[layer + 1].astype(F32)
+        DZ[layer, t] = dyv.astype(BF)
+        gather_start(DZ.at[layer], c)
+        SGV[layer, 5:6, :] = column_sum(dyv)
+
+        @pl.when(done)
+        def _():
+            g_make(first)
+
+        def feed(k, i):
+            u = UF[u_rows(layer, i), :]
+            square = u * u
+            th = jnp.tanh(GELU_K * (u + 0.044715 * (square * u)))
+            slope = 0.5 * (1.0 + th) + (0.5 * GELU_K) * u * (1.0 - th * th) * (1.0 + 0.134145 * square)
+            du = (dot_nt(DZ[layer, i], w_down(layer)) * slope).astype(BF)
+            DU[layer, i] = du
+            SBU[layer] += column_sum(du.astype(F32))
+            reduce_put(c, k, dot_nt(du, w_up(layer)))
+
+        def fold_first(k):
+            for n in range(3):
+                at_step(k, done, n + 1, lambda n=n: g_fold(first, n))
+
+        each_item(DZ.at[layer], c, feed, fold_first)
+        share(layer, (4, 6))
+
+        @pl.when(done)
+        def _():
+            g_total(second)
+
+        dc = reduce_end(c)
+        normed, scale = rows_norm(HM[layer])
+        SGV[layer, 2:3, :] = column_sum(dc * normed)
+        SGV[layer, 3:4, :] = column_sum(dc)
+        dh = valid * DY[layer + 1].astype(F32) + norm_back(dc, normed, scale, row(layer, 2))
+        DH[...] = dh
+        dattn = dh.astype(BF)
+        DAT[layer, t] = dattn
+        gather_start(DAT.at[layer], c + 1)
+        SGV[layer, 4:5, :] = column_sum(dattn.astype(F32))
+
+        @pl.when(mine)
+        def _():
+            g_make(second)
+
+        def attend(k, i):
+            dmixed = dot_nt(DAT[layer, i], w_out(layer)).astype(BF)
+            qkv = QKV[layer, i]
+            probs = PR[layer, i]
+            stack = split_heads(dmixed, heads, HD)
+            dprobs = dot_nt(stack, qkv[:, 2 * wide :])
+            dscores = (probs * (dprobs - jnp.sum(probs * dprobs, axis=-1, keepdims=True))).astype(BF)
+            DS[layer] += dscores.astype(F32)
+            dq = join_heads(dot(dscores, qkv[:, wide : 2 * wide]), heads, HD) * (HD ** (-0.5))
+            dk = dot_tn(dscores, split_heads(qkv[:, :wide], heads, HD)) * (HD ** (-0.5))
+            dv = dot_tn(probs.astype(BF), stack)
+            DQ[layer, i, :, :wide] = dq.astype(BF)
+            DQ[layer, i, :, wide : 2 * wide] = dk.astype(BF)
+            DQ[layer, i, :, 2 * wide :] = dv.astype(BF)
+            reduce_put(c + 1, k, dot_nt(DQ[layer, i], w_qkv(layer)))
+
+        def fold_second(k):
+            for n in range(4):
+                at_step(k, mine, n, lambda n=n: g_fold(second, n))
+
+        each_item(DAT.at[layer], c + 1, attend, fold_second)
+        share(layer, (5, 7))
+        da = reduce_end(c + 1)
+        normed, scale = rows_norm(XIN[layer].astype(F32))
+        SGV[layer, 0:1, :] = column_sum(da * normed)
+        SGV[layer, 1:2, :] = column_sum(da)
+        dx = DH[...] + norm_back(da, normed, scale, row(layer, 0))
+        low = dx.astype(BF)
+        DY[layer] = low
+        result = jnp.where(layer == 1, low.astype(F32), dx)
+
+        @pl.when(mine)
+        def _():
+            ig[s] = result
+
+        @pl.when(s != layer)
+        def _():
+            OWN[...] = result
+            cp = remote(OWN, ig.at[s], ss_o.at[1], rs_o.at[1], sib)
+            cp.start()
+            cp.wait_send()
+
+        return carry
+
+    lax.fori_loop(0, 2, backward, 0)
+
+    @pl.when(s == 0)
+    def _():
+        g_make(first)
+
+    spread = []
+    for i in range(2):
+        turned = skew(jnp.concatenate([DS[i], jnp.zeros((heads * rows, 128 - rows), F32)], axis=1), rows, -1)
+        table = jnp.zeros((128, 128), F32)
+        for hh in range(2):
+            for yy in range(2):
+                n = 2 * hh + yy
+                line = column_sum(turned[n * rows : (n + 1) * rows])
+                head = x + 2 * yy + 4 * z + 8 * hh
+                table = jnp.where(lanes_of((128, 128), 0) == head, line, table)
+        spread.append(
+            lax.dot_general(
+                onehot, table, (((1,), (1,)), ((), ())), precision=highest, preferred_element_type=F32
+            )
+        )
+    for hh in range(2):
+        for zz in range(2):
+            for yy in range(2):
+                j = yy + 2 * zz + 4 * hh
+                for i in range(2):
+                    MT[hh, zz, yy, i, 0:6, :] = SGV[i, 0:6, 128 * j : 128 * j + 128]
+                    for xx in range(2):
+                        for r in range(2):
+                            at = (2 * hh + yy) * block + 128 * r
+                            n = 6 + 2 * xx + r
+                            MT[hh, zz, yy, i, n : n + 1, :] = jnp.where(
+                                jnp.logical_and(z == zz, x == xx), SBU[i, :, at : at + 128], zero
+                            )
+                    MT[hh, zz, yy, i, 10:12, :] = jnp.zeros((2, 128), F32)
+                    MT[hh, zz, yy, i, 12:16, :] = spread[i][4 * j : 4 * j + 4]
+
+    def merge(n, send, keep, land, device):
+        cp = remote(send, land, ss_m.at[n], rs_m.at[n], device)
+        cp.start()
+        cp.wait()
+        keep[...] += land[...]
+
+    @pl.when(s == 0)
+    def _():
+        for c in range(first.chunks):
+            g_fold(first, c)
+
+    merge(0, MT.at[1 - h], MT.at[h], MR.at[0], hpeer)
+    merge(1, MT.at[h, 1 - z], MT.at[h, z], MR.at[1, 0], p.team(2)[0])
+    merge(2, MT.at[h, z, 1 - y], MT.at[h, z, y], MR.at[1, 1, 0], ypeer)
+    merge(3, MT.at[h, z, y, 1 - s], MT.at[h, z, y, s], MR.at[1, 1, 1, 0], sib)
+    last = remote(MT.at[h, z, y, s], MR.at[1, 1, 1, 1], ss_m.at[4], rs_m.at[4], p.team(1)[0])
+    last.start()
+    last.wait()
+    OT[...] = MT[h, z, y, s] + MR[1, 1, 1, 1]
+
+    @pl.when(s == 0)
+    def _():
+        g_total(second)
+
+    g_total(first)
+    g_end(second)
+    g_end(first)
+
+    for part in (first, second):
+        for k in (1, 2, 3):
+            w_team(part, k).wait_send()
+            g_t(part, k).wait_send()
+        for c in range(part.chunks):
+            w_h(part, c).wait_send()
+            g_h(part, c).wait_send()
+            for n in range(2):
+                w_y(part, c, n).wait_send()
+                g_y(part, c, n).wait_send()
+            for n in range(4):
+                w_s(part, c, n // 2, n % 2).wait_send()
+    for i in range(8):
+        share_copy(i, 1 - s).wait_send()
+    remote(XIN.at[1], lo.at[1 - s], ss_o.at[0], rs_o.at[0], sib).wait()
+    remote(OWN, ig.at[1 - s], ss_o.at[1], rs_o.at[1], sib).wait_recv()
+
+
+def finish_kernel(lo_in, ig_in, OQ, OO, OU, OD, OT, half, lo, ig, oq, oo, ou, od, a0, a1, a2, a3, a4, bu, a5, tab):
+    lo[...] = lo_in[...]
+    ig[...] = ig_in[...]
+    oo[...] = OO[...]
+    od[...] = OD[...]
+    block = OD.shape[0]
+    for hh in range(2):
+        for zz in range(2):
+            for yy in range(2):
+                n = 2 * hh + yy
+                d = 2 * yy + 4 * zz + 8 * hh
+                for i in range(3):
+                    at = i * 4 * HD + n * HD
+                    to = i * 16 * HD + d * HD
+                    oq[:, to : to + 2 * HD] = jnp.concatenate(
+                        [OQ[2 * zz, :, at : at + HD], OQ[2 * zz + 1, :, at : at + HD]], axis=1
+                    )
+                for xx in range(2):
+                    ou[:, (d + xx) * block : (d + xx + 1) * block] = OU[xx + 2 * zz, :, n * block : (n + 1) * block]
+    x = half[0]
+    for i, ref in enumerate((a0, a1, a2, a3, a4, a5)):
+        ref[...] = jnp.where(x == 0, OT[i : i + 1, :HD], OT[i : i + 1, HD:])
+    for r in range(2):
+        bu[:, 128 * r : 128 * r + 128] = jnp.where(x == 0, OT[6 + r : 7 + r, :], OT[8 + r : 9 + r, :])
+    for b in range(2):
+        tab[:, 16 * b : 16 * b + 16] = jnp.where(x == 0, OT[12 + b : 13 + b, :16], OT[14 + b : 15 + b, :16])
+
+
+def vm(n=1):
+    return [pl.BlockSpec(memory_space=pltpu.VMEM)] * n
+
+
+def hb(n=1):
+    return [pl.BlockSpec(memory_space=pltpu.HBM)] * n
+
+
+def sems(*shape):
+    return pltpu.SemaphoreType.DMA(shape)
+
+
+def shape_of(dims, kind):
+    return jax.ShapeDtypeStruct(dims, kind)
+
+
+def team_local(
+    audio_in, out_grad, item_len, rel_bucket, w_qkv, w_out, w_up, w_down,
+    ln1_gain, ln1_bias, ln2_gain, ln2_bias, b_out, b_up, b_down, rel_table,
+):
+    rows, width = audio_in.shape[2], audio_in.shape[3]
+    part = w_qkv.shape[1]
+    hidden = w_up.shape[2]
+    block = hidden // 16
+    wide, ff = width // 4, hidden // 4
+    low = lambda *dims: pltpu.VMEM(dims, BF)
+    full = lambda *dims: pltpu.VMEM(dims, F32)
+
+    lo, ig, OQ, OO, OU, OD, OT = pl.pallas_call(
+        step_kernel,
+        out_shape=(
+            shape_of((2, rows, width), BF),
+            shape_of((2, rows, width), F32),
+            shape_of((4, part, 3 * wide), F32),
+            shape_of((part, width), F32),
+            shape_of((4, part, ff), F32),
+            shape_of((block, width), F32),
+            shape_of((16, 128), F32),
+        ),
+        in_specs=vm(4) + hb(4) + vm(8),
+        out_specs=tuple(vm(7)),
+        scratch_shapes=[
+            low(4, part, 3 * wide), low(4, part, ff),
+            low(2, 2, 2, 2, 2, part, 3 * wide), low(2, 4, part, width),
+            low(2, 2, 2, 2, 2, part, ff), low(2, 4, block, width),
+            low(3, rows, width), low(3, rows, width),
+            low(2, 4, rows, width), low(2, 4, rows, width), low(2, 4, rows, ff), low(2, 4, rows, wide),
+            low(2, 4, rows, 3 * wide), full(2, 4, 4 * rows, rows), full(8 * rows, ff), full(2, rows, width),
+            low(2, 4, rows, width), low(2, 4, rows, width), low(2, 4, rows, ff), low(2, 4, rows, 3 * wide),
+            low(4, rows, width), low(4, rows, width), low(4, rows, ff), low(4, rows, wide),
+            low(4, rows, width), low(4, rows, width), low(4, rows, ff), low(4, rows, 3 * wide),
+            low(4, rows, width), low(4, rows, width), full(rows, width), full(rows, width),
+            low(2, 2, 2, 2, part, 3 * wide), low(4, part, width), low(2, 2, 2, 2, part, ff), low(4, block, width),
+            low(2, 2, 2, part, 3 * wide), low(2, part, width), low(2, 2, 2, part, ff), low(2, block, width),
+            low(2, 2, part, 3 * wide), low(part, width), low(2, 2, part, ff), low(block, width),
+            low(2, 2, part, 3 * wide), low(part, width), low(2, 2, part, ff), low(block, width),
+            low(4, part, 3 * wide), low(4, part, 3 * wide), low(4, part, ff), low(4, part, ff),
+            full(2, 2, 2, 2, 16, 128), full(2, 16, 128), full(2, 8, width), full(4, 8, 128),
+            full(2, 4 * rows, rows), full(128, 128), full(2, 8, width), full(2, 1, ff), full(2, 4 * rows, rows),
+            full(2, 2, 2, 2, 16, 128), full(2, 2, 2, 2, 16, 128),
+            sems(9), sems(2, 4), sems(2, 4), sems(2, 2, 4), sems(2, 2, 4), sems(2, 4), sems(2, 4),
+            sems(2, 4, 4), sems(2, 4, 4), sems(5), sems(5),
+            sems(8, 4), sems(8, 4), sems(8, 4), sems(8, 4), sems(8), sems(8), sems(2), sems(2),
+            sems(2, 2, 4), sems(2, 2, 4), sems(2, 4), sems(2, 4), sems(2, 4), sems(2, 4), sems(5), sems(5),
+        ],
+        compiler_params=pltpu.CompilerParams(
+            collective_id=0, has_side_effects=True, vmem_limit_bytes=63 << 20
+        ),
+        name="two_layers",
+    )(
+        audio_in.reshape(2, rows, width), out_grad.reshape(2, rows, width), item_len, rel_bucket[None],
+        w_qkv[0], w_out[0], w_up[0], w_down[0],
+        ln1_gain, ln1_bias, ln2_gain, ln2_bias, b_out, b_down, b_up, rel_table,
+    )
+
+    half = (lax.axis_index("dp") % 2).reshape(1)
+    lo, ig, oq, oo, ou, od, a0, a1, a2, a3, a4, bu, a5, tab = pl.pallas_call(
+        finish_kernel,
+        out_shape=(
+            shape_of((2, rows, width), BF),
+            shape_of((2, rows, width), F32),
+            shape_of((part, 3 * width), F32),
+            shape_of((part, width), F32),
+            shape_of((part, hidden), F32),
+            shape_of((block, width), F32),
+        )
+        + (shape_of((1, part), F32),) * 5
+        + (shape_of((1, block), F32), shape_of((1, part), F32), shape_of((1, 32), F32)),
+        in_specs=vm(7) + [pl.BlockSpec(memory_space=pltpu.SMEM)],
+        out_specs=tuple(vm(14)),
+        compiler_params=pltpu.CompilerParams(vmem_limit_bytes=32 << 20),
+        name="finish",
+    )(lo, ig, OQ, OO, OU, OD, OT, half)
+    return (
+        lo[None, :, None], ig[None, :, None], oq[None], oo[None], ou[None], od[None],
+        a0, a1, a2, a3, a4, bu, a5, tab,
+    )
+
+
 def solution(mesh):
+    fits = mesh.shape["dp"] == 16 and mesh.shape["section"] == 2
     return jax.shard_map(
-        local,
+        team_local if fits else local,
         mesh=mesh,
         in_specs=(
             P(None, "dp", None, None),

time: 1680 us -> 309 us (0.18)
  waiting for transfers between devices: 1190 us -> 0 us
  Pallas kernels: 0 us -> 299 us
  blocking collectives: 189 us -> 0 us
  matrix products: 148 us -> 0 us
  other arithmetic: 52.8 us -> 0 us
  local copies, waits for them, and re-layouts: 51.4 us -> 8.64 us
  between operations: 18.5 us -> 0.84 us
    reduce_scatter x4 -> x0, waiting for transfers between devices: 884 us -> none  [the longest x1 355 us: local(): lax.psum_scatter(totals[3], 'dp', scatter_dimension=0, tiled=True)]
    pallas_call x0 -> x2, Pallas kernels: none -> 299 us  [the longest x1 297 us: team_local(): pl.pallas_call(step_kernel, out_shape=(shape_of((2, rows, width), BF), sh...]
    all_gather x4 -> x0, waiting for transfers between devices: 263 us -> none  [the longest x1 114 us: local(): lax.all_gather(up_part, 'dp', axis=0, tiled=True)]
    dot_general x43 -> x0, matrix products: 148 us -> none  [the longest x8 40.4 us: contract_cols(): lax.dot_general(left, right, (((1,), (1,)), ((), ())), preferred_element_...]
    all_gather x2 -> x0, blocking collectives: 115 us -> none  [the longest x1 79 us: local(): lax.all_gather(gain_one_part, 'dp', axis=0, tiled=True)]
    unnamed x1 -> x0, blocking collectives: 74.5 us -> none
    ppermute x4 -> x0, waiting for transfers between devices: 43.4 us -> none  [passed_along(): return lax.ppermute(block, axis, route)]
  transfers between devices with their start and end apart: 12 -> 0, of which waited for: 10 -> 0; matrix products, arithmetic and copies ran while one was open for 4% -> 0% of each run, Pallas kernels for 0% -> 0%
where the time goes in v2:
time: 309 us
  Pallas kernels  299 us (97%)
  local copies, waits for them, and re-layouts  8.64 us (3%)
    pallas_call x1, Pallas kernels, team_local(): pl.pallas_call(step_kernel, out_shape=(shape_of((2, rows, width), BF), sh...  297 us
    unnamed x17, local copies, waits for them, and re-layouts  8.64 us

profile of v2, /device:TPU:0, one launch (start us, length us, event | category | flops | bytes accessed | tf_op | source)
XLA Modules:
  0.0 308.8 jit_solution(14958556385178307104)
XLA Ops:
  0.7 0.0 copy-start.7
  0.7 0.6 copy-done.7
  1.3 0.6 copy.30.il_ref
  2.0 296.9 %two_layers.1 = (bf16[2,96,1024]{2,1,0:T(8,128)(2,1)}, f32[2,96,1024]{2,1,0:T(8,128)}, f32[4,64,768]{2,1,0:T(8,128)}, f32[64,1024]{1,0:T(8,128)}, f32[4,64,1024]...) custom-call(bf16[2,96,1024]{2,1,0:T(8,128)(2,1)} %bitcast.21, bf16[2,96,1024]{2,1,0:T(8,128)(2,1)} %bitcast.22, ...), custom_call_target="tpu_custom_call" | custom-call | tf_op jit(solution)/shard_map/two_layers/pallas_call | solution.py:1288
  298.9 0.0 copy-start.6
  298.9 0.7 copy-done.6
  299.6 0.0 copy-start
  299.6 1.2 copy-done
  300.8 0.0 copy-start.1
  300.8 1.2 copy-done.1
  302.0 0.0 copy-start.2
  302.0 1.1 copy-done.2
  303.2 0.0 copy-start.3
  303.2 1.1 copy-done.3
  304.3 0.0 copy-start.4
  304.3 1.0 copy-done.4
  305.3 0.0 copy-start.5
  305.3 0.9 copy-done.5
  306.3 2.3 finish.1
Async XLA Ops:
  0.7 0.7 copy-start.7
  298.9 0.7 copy-start.6
  299.6 1.2 copy-start
  300.8 1.2 copy-start.1
  302.0 1.1 copy-start.2
  303.2 1.1 copy-start.3
  304.3 1.0 copy-start.4
  305.3 0.9 copy-start.5

commit v3 on v2

--- a/solution.py
+++ b/solution.py
@@ -554,10 +554,10 @@
     x_ref, og_ref, il_ref, rb_ref, wq_in, wo_in, wu_in, wd_in,
     v0_ref, v1_ref, v2_ref, v3_ref, v4_ref, v5_ref, bu_ref, rt_ref,
     lo, ig, OQ, OO, OU, OD, OT,
-    SQ, SU, WQ, WO, WU, WD, XIN, DY, A, C, FA, MIX, QKV, PR, UF, HM, DZ, DAT, DU, DQ,
-    XA, XC, XF, XM, XDZ, XDAT, XDU, XDQ, RB, SB, OWN, DH,
-    GQ, GO, GU, GD, YQ, YO, YU, YD, ZSQ, ZSO, ZSU, ZSD, ZRQ, ZRO, ZRU, ZRD, TSQ, TRQ, TSU, TRU,
-    SPT, SPX, VEC, LEN, BIAS, PD, SGV, SBU, DS, MT, MR,
+    SQ, SU, WQ, WO, WU, WD, XG, XIN, A, C, FA, MIX, QKV, PR, UF, HM, DZ, DAT, DU, DQ,
+    XA, XC, XF, XM, XDZ, XDAT, XDU, XDQ, RB, SB, OWN, OWNY, DX, DH,
+    GQ, GO, GU, GD, YQ, YO, YU, YD, ZSQ, ZSO, ZSU, ZSD, ZRQ, ZRO, ZRU, ZRD, TRQ, TRU,
+    SPT, SPR, VEC, LEN, BIAS, PD, SGV, SBU, DS, MT, MR, M1, MN,
     ls, ss_a, rs_a, ss_wy, rs_wy, ss_wh, rs_wh, ss_ws, rs_ws, ss_p, rs_p,
     ss_g, rs_g, ss_r, rs_r, ss_x, rs_x, ss_o, rs_o,
     ss_gy, rs_gy, ss_gh, rs_gh, ss_gt, rs_gt, ss_m, rs_m,
@@ -572,10 +572,108 @@
     part_rows = WO.shape[2]
     block = WD.shape[2]
 
+    def only(core, what):
+        @pl.when(s == core)
+        def _():
+            what()
+
+    SY, RY = DU.at[0], DAT.at[0]
+    half = rows // 2
+    upper, lower = pl.ds(0, half), pl.ds(half, half)
+    x_dev, x_slot = p.team(1)
+    z_dev, z_slot = p.team(2)
+    d_slot = p.team(3)[1]
+
+    def hop(ref, c, n, slot, span, device):
+        view = ref.at[slot, span]
+        return remote(view, view, ss_g.at[c, n], rs_g.at[c, n], device)
+
+    def gather_sends(ref, c):
+        return (
+            hop(ref, c, 2, t, upper, z_dev), hop(ref, c, 0, t, upper, x_dev),
+            hop(ref, c, 3, t, lower, z_dev), hop(ref, c, 1, t, lower, x_dev),
+        )
+
+    def relays(ref, c):
+        return hop(ref, c, 4, z_slot, upper, x_dev), hop(ref, c, 5, z_slot, lower, x_dev)
+
+    def gather_start(ref, c):
+        for cp in gather_sends(ref, c):
+            cp.start()
+
+    def gather_relay(ref, c):
+        onward = relays(ref, c)
+        hop(ref, c, 2, z_slot, upper, z_dev).wait_recv()
+        onward[0].start()
+        hop(ref, c, 3, z_slot, lower, z_dev).wait_recv()
+        onward[1].start()
+
+    def gather_take(ref, c, k):
+        if k == 1:
+            hop(ref, c, 0, x_slot, upper, x_dev).wait_recv()
+            hop(ref, c, 1, x_slot, lower, x_dev).wait_recv()
+        if k == 3:
+            hop(ref, c, 4, d_slot, upper, x_dev).wait_recv()
+            hop(ref, c, 5, d_slot, lower, x_dev).wait_recv()
+
+    def gather_end(ref, c):
+        for cp in gather_sends(ref, c) + relays(ref, c):
+            cp.wait_send()
+
+    def reduce_copy(c, k, side=False):
+        out, land = (SY, RY) if side else (SB, RB)
+        return remote(out.at[k], land.at[k], ss_r.at[c, k], rs_r.at[c, k], p.team(k)[0])
+
+    def reduce_put(c, k, value, side=False):
+        @pl.when(k == 0)
+        def _():
+            (OWNY if side else OWN)[...] = value
+
+        @pl.when(k > 0)
+        def _():
+            (SY if side else SB)[k] = value.astype(BF)
+            reduce_copy(c, k, side).start()
+
+    def reduce_end(c, side=False):
+        total = (OWNY if side else OWN)[...]
+        for k in (1, 2, 3):
+            reduce_copy(c, k, side).wait()
+            total = total + (RY if side else RB)[k].astype(F32)
+        return total
+
+    def each_item(gathers, body, aside, relay=True):
+        def step(n, carry):
+            if relay:
+
+                @pl.when(n == 1)
+                def _():
+                    gather_relay(*gathers[0])
+
+            for m, mate in ((2, 1), (3, 3)):
+
+                @pl.when(n == m)
+                def _(mate=mate):
+                    for ref, c in gathers:
+                        gather_take(ref, c, mate)
+
+            k = 2 * (n % 2) + n // 2
+            body(k, p.team(k)[1])
+            aside(n)
+            return carry
+
+        lax.fori_loop(0, 4, step, 0)
+        for ref, c in gathers:
+            gather_end(ref, c)
+
+    def at_step(k, here, n, what):
+        @pl.when(jnp.logical_and(here, k == n))
+        def _():
+            what()
+
     first = Part(0, 1, W=WQ, V=WO, S=SQ, G=GQ, R=GO, Y=YQ, YR=YO, ZS=ZSQ, ZSR=ZSO, ZR=ZRQ, ZRR=ZRO,
-                 TS=TSQ, TR=TRQ, O=OQ, OR=OO)
+                 TS=SQ, TR=TRQ, O=OQ, OR=OO)
     second = Part(1, 2, W=WU, V=WD, S=SU, G=GU, R=GD, Y=YU, YR=YD, ZS=ZSU, ZSR=ZSD, ZR=ZRU, ZRR=ZRD,
-                  TS=TSU, TR=TRU, O=OU, OR=OD)
+                  TS=SU, TR=TRU, O=OU, OR=OD)
 
     loads = [
         pltpu.make_async_copy(wq_in.at[:, pl.ds(width * i, width)], UF.at[pl.ds(576 + 64 * i, 64)], ls.at[i])
@@ -587,11 +685,18 @@
         for i in range(4)
     ]
     loads.append(pltpu.make_async_copy(wd_in, UF.at[pl.ds(64, 256)], ls.at[8]))
+    loads.append(pltpu.make_async_copy(x_ref.at[s], XG.at[t], ls.at[9]))
+    loads.append(pltpu.make_async_copy(og_ref.at[s], DZ.at[1, t], ls.at[10]))
     for cp in loads:
         cp.start()
 
     bell = pltpu.get_barrier_semaphore()
-    everyone = (sib, p.team(1)[0], p.team(2)[0], p.team(3)[0], ypeer, hpeer)
+    around = [(a, b, e) for a in range(2) for b in range(2) for e in range(2)][1:]
+
+    def station(a, b, e):
+        return p.device(s=s + a * (1 - 2 * s), y=y + b * (1 - 2 * y), h=h + e * (1 - 2 * h))
+
+    everyone = [p.team(k)[0] for k in (1, 2, 3)] + [station(*o) for o in around]
     for peer in everyone:
         pl.semaphore_signal(bell, inc=1, device_id=peer, device_id_type=MESH)
 
@@ -635,23 +740,31 @@
         n = 2 * hh + yy
         return remote(view, view, ss_ws.at[part.index, n, c], rs_ws.at[part.index, n, c], sib)
 
-    def w_spread(part):
-        for k in (1, 2, 3):
-            w_team(part, k).wait_recv()
-        for c in range(part.chunks):
-            w_h(part, c).start()
-            w_y(part, c, 0).start()
-            w_s(part, c, h, y).start()
-
-    def w_pass(part, c):
+    order = ((first, 2), (first, 0), (first, 1), (second, 0), (second, 1), (second, 2), (second, 3))
+
+    def w_share(j):
+        part, c = order[j]
+        if j in (1, 3):
+            for k in (1, 2, 3):
+                w_team(part, k).wait_recv()
+        w_h(part, c).start()
+        w_y(part, c, 0).start()
+        w_s(part, c, h, y).start()
+
+    def w_pass(j):
+        part, c = order[j]
         w_h(part, c).wait_recv()
         w_y(part, c, 1).start()
         w_s(part, c, 1 - h, y).start()
-
-    def w_last(part):
+        if j + 2 < len(order):
+            w_share(j + 2)
+
+    def w_near(part):
         for c in range(part.chunks):
             w_y(part, c, 0).wait_recv()
             w_s(part, c, h, 1 - y).start()
+
+    def w_far(part):
         for c in range(part.chunks):
             w_y(part, c, 1).wait_recv()
             w_s(part, c, 1 - h, 1 - y).start()
@@ -663,7 +776,13 @@
 
     for k in (1, 2, 3):
         w_team(first, k).start()
-    for cp in loads[4:]:
+    loads[9].wait()
+
+    @pl.when(s == 0)
+    def _():
+        w_share(0)
+
+    for cp in loads[4:9]:
         cp.wait()
     for hh in range(2):
         for zz in range(2):
@@ -675,12 +794,12 @@
                     SU[xx + 2 * zz, :, at : at + block] = UF[low : low + 64, col : col + block].astype(BF)
     WU[s, h, z, y, x] = SU[t]
     WD[s, q] = UF[64 : 64 + block, :].astype(BF)
-    for k in (1, 2, 3):
-        w_team(second, k).start()
-
-    @pl.when(s == 0)
-    def _():
-        w_spread(first)
+
+    position = lanes_of((rows, 1), 0).astype(F32)
+    count = jnp.where(s == 0, il_ref[0:1, :], il_ref[1:2, :]).astype(F32)
+    valid = (position < count).astype(F32)
+    loads[10].wait()
+    DZ[1, t] = (valid * DZ[1, t].astype(F32)).astype(BF)
 
     lane = lanes_of((1, 128))
     zero = jnp.zeros((1, 128), F32)
@@ -697,24 +816,37 @@
     for i in range(2):
         lines.append(zero)
     for i in range(16):
-        SPX[0, i : i + 1, :] = lines[i].astype(BF).astype(F32)
-
-    def swap(n, src, dst, device):
-        cp = remote(src, dst, ss_p.at[n], rs_p.at[n], device)
-        cp.start()
-        cp.wait()
-
-    swap(0, SPX.at[0], SPX.at[1], p.team(1)[0])
-    SPT[h, z, y, s] = SPX[0] + SPX[1]
-    for n, (view, device) in enumerate(
-        (
-            (SPT.at[h, z, y, s], sib),
-            (SPT.at[h, z, y], ypeer),
-            (SPT.at[h, z], p.team(2)[0]),
-            (SPT.at[h], hpeer),
-        )
-    ):
-        swap(n + 1, view, view, device)
+        SPR[t, h, y, s, i : i + 1, :] = lines[i].astype(BF).astype(F32)
+
+    def near_copy(n):
+        view = SPR.at[t, h, y, s]
+        return remote(view, view, ss_p.at[n], rs_p.at[n], station(*around[n]))
+
+    def team_copy(k):
+        view = SPR.at[t]
+        return remote(view, view, ss_p.at[6 + k], rs_p.at[6 + k], p.team(k)[0])
+
+    for n in range(7):
+        near_copy(n).start()
+    only(0, lambda: w_share(1))
+    gather_start(XG, 0)
+    for n in range(7):
+        near_copy(n).wait()
+    for k in (1, 2, 3):
+        team_copy(k).start()
+    for k in (1, 2, 3):
+        w_team(second, k).start()
+    only(0, lambda: w_pass(0))
+    gather_relay(XG, 0)
+    for k in (1, 2, 3):
+        team_copy(k).wait()
+    for hh in range(2):
+        for zz in range(2):
+            for yy in range(2):
+                for i in range(2):
+                    SPT[hh, zz, yy, i] = SPR[2 * zz, hh, yy, i] + SPR[2 * zz + 1, hh, yy, i]
+    gather_start(DZ.at[1], 4)
+    only(0, lambda: (w_pass(1), w_pass(2)))
 
     for hh in range(2):
         for zz in range(2):
@@ -732,8 +864,8 @@
     for zz in range(2):
         tile = SPT[h, zz, y, 0]
         for xx in range(2):
-            count = jnp.sum(jnp.where(lane == s, tile[12 + xx : 13 + xx], 0.0), axis=1, keepdims=True)
-            LEN[xx + 2 * zz] = jnp.broadcast_to(count, (8, 128))
+            tokens = jnp.sum(jnp.where(lane == s, tile[12 + xx : 13 + xx], 0.0), axis=1, keepdims=True)
+            LEN[xx + 2 * zz] = jnp.broadcast_to(tokens, (8, 128))
 
     mark = jnp.concatenate([rb_ref[...], jnp.full((1, 128 - rows), 2 * NB, jnp.int32)], axis=1).astype(BF)
     mark = jnp.broadcast_to(mark, (8, 128))
@@ -759,72 +891,18 @@
         grid = skew(jnp.concatenate(stack, axis=0), rows, 1)[:, :rows]
         causal = lanes_of(grid.shape) <= lanes_of(grid.shape, 0) % rows
         BIAS[i] = jnp.where(causal, grid, -1000000000.0)
-
-    def gather_copy(ref, c, k):
-        return remote(ref.at[t], ref.at[t], ss_g.at[c, k], rs_g.at[c, k], p.team(k)[0])
-
-    def gather_start(ref, c):
-        gather_copy(ref, c, 1).start()
-        gather_copy(ref, c, 2).start()
-
-    def gather_take(ref, c, k):
-        device, slot = p.team(k)
-        remote(ref.at[slot], ref.at[slot], ss_g.at[c, k], rs_g.at[c, k], device).wait_recv()
-
-    def reduce_copy(c, k):
-        return remote(SB.at[k], RB.at[k], ss_r.at[c, k], rs_r.at[c, k], p.team(k)[0])
-
-    def reduce_put(c, k, value):
-        @pl.when(k == 0)
-        def _():
-            OWN[...] = value
-
-        @pl.when(k > 0)
-        def _():
-            SB[k] = value.astype(BF)
-            reduce_copy(c, k).start()
-
-    def reduce_end(c):
-        total = OWN[...]
-        for k in (1, 2, 3):
-            reduce_copy(c, k).wait()
-            total = total + RB[k].astype(F32)
-        return total
-
-    def each_item(ref, c, body, aside):
-        def step(k, carry):
-            @pl.when(k > 0)
-            def _():
-                gather_take(ref, c, k)
-
-            body(k, p.team(k)[1])
-
-            @pl.when(k == 0)
-            def _():
-                gather_copy(ref, c, 3).start()
-
-            aside(k)
-            return carry
-
-        lax.fori_loop(0, 4, step, 0)
-        for k in (1, 2, 3):
-            gather_copy(ref, c, k).wait_send()
-
-    def at_step(k, here, n, what):
-        @pl.when(jnp.logical_and(here, k == n))
-        def _():
-            what()
+    gather_relay(DZ.at[1], 4)
 
     pairs = ((A, XA), (MIX, XM), (C, XC), (FA, XF), (DZ, XDZ), (DAT, XDAT), (DU, XDU), (DQ, XDQ))
 
-    def share_copy(i, layer):
-        return remote(pairs[i][0].at[layer], pairs[i][1], ss_x.at[i], rs_x.at[i], sib)
-
-    def share(layer, which):
+    def share_copy(i, layer, slot):
+        return remote(pairs[i][0].at[layer, slot], pairs[i][1].at[slot], ss_x.at[i, slot], rs_x.at[i, slot], sib)
+
+    def share_item(k, layer, which):
         @pl.when(s != layer)
         def _():
             for i in which:
-                share_copy(i, layer).start()
+                share_copy(i, layer, p.team(k)[1]).start()
 
     def row(layer, index):
         return VEC[layer, index : index + 1, :]
@@ -843,9 +921,6 @@
 
     def u_rows(layer, i):
         return pl.ds(pl.multiple_of((layer * 4 + i) * rows, 8), rows)
-
-    position = lanes_of((rows, 1), 0).astype(F32)
-    valid = (position < LEN[t][0:1, 0:1]).astype(F32)
 
     def g_own(part, c, hh, yy):
         if c < 2:
@@ -859,6 +934,12 @@
 
     def g_half(n):
         return (1 - h) + n * (2 * h - 1)
+
+    def g_big(part, c, n):
+        return remote(
+            part.G.at[g_half(n), c, 1 - y], part.Y.at[n, c],
+            ss_gy.at[part.index, n, c], rs_gy.at[part.index, n, c], ypeer,
+        )
 
     def g_y(part, c, n):
         return remote(
@@ -891,7 +972,7 @@
             flat(left[1], span), flat(right[1], every)
         )
 
-    def g_make(part):
+    def g_make(part, n):
         if part is first:
             need = (0, 1, 5, 7)
             big_l, big_r = (A.at[s], XA), (DQ.at[s], XDQ)
@@ -902,32 +983,45 @@
             big_l, big_r = (C.at[s], XC), (DU.at[s], XDU)
             small_l, small_r = (FA.at[s], XF), (DZ.at[s], XDZ)
             small_span = block
-        for i in need:
-            share_copy(i, s).wait_recv()
+        if n == 0:
+            for i in need:
+                for slot in range(4):
+                    share_copy(i, s, slot).wait_recv()
+        hh = g_half(n)
         if part is first:
-            value = product(small_l, small_r, pl.ds(0, wide)).astype(BF)
-            for i in range(4):
-                part.R[i] = value[i * small_span : (i + 1) * small_span]
-
-        def tile(n, carry):
-            hh = g_half(n)
-            for zz in range(2):
-                span = pl.ds(pl.multiple_of((2 * hh + zz) * 256, 256), 256)
-                value = product(big_l, big_r, span).astype(BF)
-                part.G[hh, zz] = value.reshape(2, 2, part_rows, value.shape[1])
-                g_y(part, zz, n).start()
-            if part is second:
-                for yy in (1 - y, y):
-                    span = pl.ds(pl.multiple_of((2 * hh + yy) * 256, 256), 256)
-                    part.R[2 * hh + yy] = product(small_l, small_r, span).astype(BF)
-                    if yy is not y:
+            if n == 0:
+                value = product(small_l, small_r, pl.ds(0, wide)).astype(BF)
+                for i in range(4):
+                    part.R[i] = value[i * small_span : (i + 1) * small_span]
+            if n == 0:
+                g_y(part, 2, n).start()
+
+        def tile(zz, carry):
+            span = pl.ds(pl.multiple_of((2 * hh + zz) * 256, 256), 256)
+            value = product(big_l, big_r, span).astype(BF)
+            part.G[hh, zz] = value.reshape(2, 2, part_rows, value.shape[1])
+            if n == 0:
+                g_big(part, zz, n).start()
+            return carry
+
+        lax.fori_loop(0, 2, tile, 0)
+        if part is second:
+
+            def strip(m, carry):
+                yy = (1 - y) + m * (2 * y - 1)
+                span = pl.ds(pl.multiple_of((2 * hh + yy) * 256, 256), 256)
+                part.R[2 * hh + yy] = product(small_l, small_r, span).astype(BF)
+
+                if n == 0:
+
+                    @pl.when(m == 0)
+                    def _():
                         for c in range(2, part.chunks):
                             g_y(part, c, n).start()
-            else:
-                g_y(part, 2, n).start()
-            return carry
-
-        lax.fori_loop(0, 2, tile, 0)
+
+                return carry
+
+            lax.fori_loop(0, 2, strip, 0)
 
     def g_fold(part, c):
         g_y(part, c, 0).wait_recv()
@@ -936,6 +1030,10 @@
         ).astype(BF)
         g_h(part, c).start()
 
+    def g_later(part):
+        for c in range(part.chunks):
+            g_y(part, c, 1).start()
+
     def g_total(part):
         for c in range(part.chunks):
             g_y(part, c, 1).wait_recv()
@@ -957,33 +1055,26 @@
             g_t(part, k).wait_recv()
             part.O[p.team(k)[1]] = part.TR[k].astype(F32)
 
-    XIN[0] = x_ref[s]
-    DY[2] = og_ref[s]
-
-    @pl.when(s == 0)
-    def _():
-        for c in range(first.chunks):
-            w_pass(first, c)
-        w_spread(second)
-
-    def forward(layer, carry):
-        mine = s == layer
-        coming = jnp.logical_and(s == 1, layer == 0)
-        xin = XIN[layer].astype(F32)
-        normed, _ = rows_norm(xin)
-        A[layer, t] = (normed * row(layer, 0) + row(layer, 1)).astype(BF)
-        c = 2 * layer
-        gather_start(A.at[layer], c)
-
-        @pl.when(mine)
-        def _():
-            w_last(first)
-
-        @pl.when(s != layer)
-        def _():
-            w_other(first)
+    XIN[0] = XG[t]
+    DS[...] = jnp.zeros_like(DS)
+    SBU[...] = jnp.zeros_like(SBU)
+    SGV[...] = jnp.zeros_like(SGV)
+
+    def scaled(value, layer, at):
+        return (rows_norm(value)[0] * row(layer, at) + row(layer, at + 1)).astype(BF)
+
+    def attention(layer):
+        if layer == 1:
+            A[layer, t] = scaled(XIN[layer].astype(F32), layer, 0)
+            gather_start(A.at[layer], 2)
+        if layer == 0:
+            only(0, lambda: w_near(first))
+        only(layer, lambda: w_far(first))
+        only(1 - layer, lambda: w_other(first))
 
         def attend(k, i):
+            if layer == 0:
+                A[layer, i] = scaled(XG[i].astype(F32), layer, 0)
             qkv = dot(A[layer, i], w_qkv(layer)).astype(BF)
             QKV[layer, i] = qkv
             stack = split_heads(qkv[:, :wide], heads, HD)
@@ -995,113 +1086,103 @@
             PR[layer, i] = probs
             mixed = join_heads(dot(probs.astype(BF), qkv[:, 2 * wide :]), heads, HD).astype(BF)
             MIX[layer, i] = mixed
-            reduce_put(c, k, dot(mixed, w_out(layer)))
+            reduce_put(2 * layer, k, dot(mixed, w_out(layer)))
 
         def pass_on(k):
-            for n in range(3):
-                at_step(k, mine, n + 1, lambda n=n: w_pass(second, n))
-
-        each_item(A.at[layer], c, attend, pass_on)
-        share(layer, (0, 1))
-        hmid = xin + reduce_end(c) + row(layer, 4)
+            if layer == 0:
+                for n in range(4):
+                    at_step(k, s == 0, n, lambda n=n: w_pass(3 + n))
+                at_step(k, s == 0, 2, lambda: w_near(second))
+                at_step(k, s == 1, 2, lambda: (w_share(0), w_share(1)))
+                at_step(k, s == 1, 3, lambda: w_pass(0))
+            else:
+                at_step(k, s == 1, 0, lambda: w_pass(6))
+                at_step(k, s == 1, 1, lambda: w_near(second))
+            share_item(2 * (k % 2) + k // 2, layer, (0, 1))
+
+        each_item(((XG, 0),) if layer == 0 else ((A.at[layer], 2),), attend, pass_on, relay=layer == 1)
+        hmid = XIN[layer].astype(F32) + reduce_end(2 * layer) + row(layer, 4)
         HM[layer] = hmid
-        normed, _ = rows_norm(hmid)
-        C[layer, t] = (normed * row(layer, 2) + row(layer, 3)).astype(BF)
-        gather_start(C.at[layer], c + 1)
-
-        @pl.when(mine)
+        C[layer, t] = scaled(hmid, layer, 2)
+        gather_start(C.at[layer], 2 * layer + 1)
+
+    def hidden_back(layer, i, u, th):
+        square = u * u
+        slope = 0.5 * (1.0 + th) + (0.5 * GELU_K) * u * (1.0 - th * th) * (1.0 + 0.134145 * square)
+        du = (dot_nt(DZ[layer, i], w_down(layer)) * slope).astype(BF)
+        DU[layer, i] = du
+        SBU[layer] += column_sum(du.astype(F32))
+        return dot_nt(du, w_up(layer))
+
+    def feed_forward(layer):
+        only(layer, lambda: w_far(second))
+        only(1 - layer, lambda: w_other(second))
+        if layer == 0:
+            only(1, lambda: w_pass(1))
+
+        def feed(k, i):
+            u = dot(C[layer, i], w_up(layer)) + row(layer, 6)
+            th = jnp.tanh(GELU_K * (u + 0.044715 * (u * u * u)))
+            if layer == 0:
+                UF[u_rows(layer, i), :] = u
+            else:
+                reduce_put(4, k, hidden_back(layer, i, u, th))
+            f = (0.5 * u * (1.0 + th)).astype(BF)
+            FA[layer, i] = f
+            reduce_put(2 * layer + 1, k, dot(f, w_down(layer)), side=layer == 1)
+
+        def prepare(k):
+            if layer == 0:
+                for n in range(4):
+                    at_step(k, s == 1, n, lambda n=n: w_pass(2 + n))
+                at_step(k, s == 1, 2, lambda: w_near(first))
+            share_item(2 * (k % 2) + k // 2, layer, (2, 3) if layer == 0 else (2, 3, 4, 6))
+
+        gathers = ((C.at[layer], 2 * layer + 1),)
+        if layer == 1:
+            gathers += ((DZ.at[layer], 4),)
+        each_item(gathers, feed, prepare)
+
+    def layer_result(layer):
+        return (valid * (HM[layer] + reduce_end(2 * layer + 1, side=layer == 1) + row(layer, 5))).astype(BF)
+
+    def give_result(layer):
+        @pl.when(s == layer)
         def _():
-            w_pass(second, 3)
-            w_last(second)
+            lo[s] = XIN[layer + 1]
 
         @pl.when(s != layer)
         def _():
-            w_other(second)
-
-        def feed(k, i):
-            u = dot(C[layer, i], w_up(layer)) + row(layer, 6)
-            UF[u_rows(layer, i), :] = u
-            f = (0.5 * u * (1.0 + jnp.tanh(GELU_K * (u + 0.044715 * (u * u * u))))).astype(BF)
-            FA[layer, i] = f
-            reduce_put(c + 1, k, dot(f, w_down(layer)))
-
-        def prepare(k):
-            at_step(k, coming, 0, lambda: w_spread(first))
-            for n in range(3):
-                at_step(k, coming, n + 1, lambda n=n: w_pass(first, n))
-            at_step(k, coming, 3, lambda: w_spread(second))
-
-        each_item(C.at[layer], c + 1, feed, prepare)
-        share(layer, (2, 3))
-        out = (valid * (HM[layer] + reduce_end(c + 1) + row(layer, 5))).astype(BF)
-        XIN[layer + 1] = out
-        return carry
-
-    lax.fori_loop(0, 2, forward, 0)
-    for layer in (0, 1):
-
-        @pl.when(s == layer)
-        def _(layer=layer):
-            lo[s] = XIN[layer + 1]
-
-        @pl.when(s != layer)
-        def _(layer=layer):
             remote(XIN.at[layer + 1], lo.at[s], ss_o.at[0], rs_o.at[0], sib).start()
 
-    DS[...] = jnp.zeros_like(DS)
-    SBU[...] = jnp.zeros_like(SBU)
-    SGV[...] = jnp.zeros_like(SGV)
-
-    def backward(back, carry):
-        layer = 1 - back
-        mine = s == layer
-        done = jnp.logical_and(s == 1, layer == 0)
-        c = 4 + 2 * back
-        dyv = valid * DY[layer + 1].astype(F32)
-        DZ[layer, t] = dyv.astype(BF)
-        gather_start(DZ.at[layer], c)
-        SGV[layer, 5:6, :] = column_sum(dyv)
-
-        @pl.when(done)
-        def _():
-            g_make(first)
-
+    def feed_back(layer):
         def feed(k, i):
             u = UF[u_rows(layer, i), :]
-            square = u * u
-            th = jnp.tanh(GELU_K * (u + 0.044715 * (square * u)))
-            slope = 0.5 * (1.0 + th) + (0.5 * GELU_K) * u * (1.0 - th * th) * (1.0 + 0.134145 * square)
-            du = (dot_nt(DZ[layer, i], w_down(layer)) * slope).astype(BF)
-            DU[layer, i] = du
-            SBU[layer] += column_sum(du.astype(F32))
-            reduce_put(c, k, dot_nt(du, w_up(layer)))
+            th = jnp.tanh(GELU_K * (u + 0.044715 * (u * u * u)))
+            reduce_put(6, k, hidden_back(layer, i, u, th))
 
         def fold_first(k):
-            for n in range(3):
-                at_step(k, done, n + 1, lambda n=n: g_fold(first, n))
-
-        each_item(DZ.at[layer], c, feed, fold_first)
-        share(layer, (4, 6))
-
-        @pl.when(done)
-        def _():
-            g_total(second)
-
-        dc = reduce_end(c)
+            for n in range(2):
+                at_step(k, s == 1, n, lambda n=n: g_fold(first, n))
+            at_step(k, s == 1, 1, lambda: g_later(first))
+            share_item(2 * (k % 2) + k // 2, layer, (4, 6))
+
+        each_item(((DZ.at[layer], 6),), feed, fold_first)
+
+    def middle_back(layer):
+        dc = reduce_end(6 - 2 * layer)
         normed, scale = rows_norm(HM[layer])
         SGV[layer, 2:3, :] = column_sum(dc * normed)
         SGV[layer, 3:4, :] = column_sum(dc)
-        dh = valid * DY[layer + 1].astype(F32) + norm_back(dc, normed, scale, row(layer, 2))
+        dh = DZ[layer, t].astype(F32) + norm_back(dc, normed, scale, row(layer, 2))
         DH[...] = dh
         dattn = dh.astype(BF)
         DAT[layer, t] = dattn
-        gather_start(DAT.at[layer], c + 1)
+        gather_start(DAT.at[layer], 7 - 2 * layer)
         SGV[layer, 4:5, :] = column_sum(dattn.astype(F32))
-
-        @pl.when(mine)
-        def _():
-            g_make(second)
-
+        only(layer, lambda: (g_make(second, 1), g_fold(second, 0), g_fold(second, 1)))
+
+    def attention_back(layer):
         def attend(k, i):
             dmixed = dot_nt(DAT[layer, i], w_out(layer)).astype(BF)
             qkv = QKV[layer, i]
@@ -1116,41 +1197,66 @@
             DQ[layer, i, :, :wide] = dq.astype(BF)
             DQ[layer, i, :, wide : 2 * wide] = dk.astype(BF)
             DQ[layer, i, :, 2 * wide :] = dv.astype(BF)
-            reduce_put(c + 1, k, dot_nt(DQ[layer, i], w_qkv(layer)))
+            reduce_put(7 - 2 * layer, k, dot_nt(DQ[layer, i], w_qkv(layer)))
 
         def fold_second(k):
-            for n in range(4):
-                at_step(k, mine, n, lambda n=n: g_fold(second, n))
-
-        each_item(DAT.at[layer], c + 1, attend, fold_second)
-        share(layer, (5, 7))
-        da = reduce_end(c + 1)
+            for n in range(2):
+                at_step(k, s == layer, n, lambda n=n: g_fold(second, n + 2))
+            at_step(k, s == layer, 1, lambda: g_later(second))
+            share_item(2 * (k % 2) + k // 2, layer, (5, 7))
+
+        each_item(((DAT.at[layer], 7 - 2 * layer),), attend, fold_second)
+
+    def inputs_back(layer):
+        da = reduce_end(7 - 2 * layer)
         normed, scale = rows_norm(XIN[layer].astype(F32))
+        dx = DH[...] + norm_back(da, normed, scale, row(layer, 0))
+        low = dx.astype(BF)
+        if layer == 1:
+            dyv = valid * low.astype(F32)
+            DZ[0, t] = dyv.astype(BF)
+            gather_start(DZ.at[0], 6)
+            SGV[0, 5:6, :] = column_sum(dyv)
         SGV[layer, 0:1, :] = column_sum(da * normed)
         SGV[layer, 1:2, :] = column_sum(da)
-        dx = DH[...] + norm_back(da, normed, scale, row(layer, 0))
-        low = dx.astype(BF)
-        DY[layer] = low
-        result = jnp.where(layer == 1, low.astype(F32), dx)
-
-        @pl.when(mine)
+        result = low.astype(F32) if layer == 1 else dx
+
+        @pl.when(s == layer)
         def _():
             ig[s] = result
 
         @pl.when(s != layer)
         def _():
-            OWN[...] = result
-            cp = remote(OWN, ig.at[s], ss_o.at[1], rs_o.at[1], sib)
-            cp.start()
-            cp.wait_send()
-
-        return carry
-
-    lax.fori_loop(0, 2, backward, 0)
-
-    @pl.when(s == 0)
-    def _():
-        g_make(first)
+            DX[...] = result
+            remote(DX, ig.at[s], ss_o.at[1], rs_o.at[1], sib).start()
+
+    attention(0)
+    feed_forward(0)
+    XIN[1] = layer_result(0)
+    attention(1)
+    give_result(0)
+    feed_forward(1)
+    for part in (first, second):
+        for k in (1, 2, 3):
+            w_team(part, k).wait_send()
+    only(1, lambda: g_make(second, 0))
+    SGV[1, 5:6, :] = column_sum(DZ[1, t].astype(F32))
+    middle_back(1)
+    XIN[2] = layer_result(1)
+    give_result(1)
+    attention_back(1)
+    only(1, lambda: g_make(first, 0))
+    inputs_back(1)
+    only(1, lambda: (g_make(first, 1), g_fold(first, 2)))
+    feed_back(0)
+    only(0, lambda: g_make(second, 0))
+    only(1, lambda: g_total(second))
+    middle_back(0)
+    attention_back(0)
+    only(0, lambda: (g_make(first, 0), g_make(first, 1)))
+    inputs_back(0)
+
+    only(0, lambda: (g_fold(first, 2), g_fold(first, 0), g_fold(first, 1), g_later(first)))
 
     spread = []
     for i in range(2):
@@ -1183,37 +1289,35 @@
                     MT[hh, zz, yy, i, 10:12, :] = jnp.zeros((2, 128), F32)
                     MT[hh, zz, yy, i, 12:16, :] = spread[i][4 * j : 4 * j + 4]
 
-    def merge(n, send, keep, land, device):
-        cp = remote(send, land, ss_m.at[n], rs_m.at[n], device)
-        cp.start()
-        cp.wait()
-        keep[...] += land[...]
-
-    @pl.when(s == 0)
-    def _():
-        for c in range(first.chunks):
-            g_fold(first, c)
-
-    merge(0, MT.at[1 - h], MT.at[h], MR.at[0], hpeer)
-    merge(1, MT.at[h, 1 - z], MT.at[h, z], MR.at[1, 0], p.team(2)[0])
-    merge(2, MT.at[h, z, 1 - y], MT.at[h, z, y], MR.at[1, 1, 0], ypeer)
-    merge(3, MT.at[h, z, y, 1 - s], MT.at[h, z, y, s], MR.at[1, 1, 1, 0], sib)
-    last = remote(MT.at[h, z, y, s], MR.at[1, 1, 1, 1], ss_m.at[4], rs_m.at[4], p.team(1)[0])
-    last.start()
-    last.wait()
-    OT[...] = MT[h, z, y, s] + MR[1, 1, 1, 1]
-
-    @pl.when(s == 0)
-    def _():
-        g_total(second)
-
+    def team_merge(k):
+        return remote(MT.at[:, p.mate(k)[1]], MR.at[k], ss_m.at[6 + k], rs_m.at[6 + k], p.team(k)[0])
+
+    def near_merge(n):
+        a, b, e = around[n]
+        there = (h + e * (1 - 2 * h), y + b * (1 - 2 * y), s + a * (1 - 2 * s))
+        return remote(M1.at[there], MN.at[n], ss_m.at[n], rs_m.at[n], station(a, b, e))
+
+    for k in (1, 2, 3):
+        team_merge(k).start()
+    only(0, lambda: g_total(second))
+    for k in (1, 2, 3):
+        team_merge(k).wait()
+    for hh in range(2):
+        M1[hh] = MT[hh, z] + MR[1, hh] + MR[2, hh] + MR[3, hh]
+    for n in range(7):
+        near_merge(n).start()
     g_total(first)
     g_end(second)
+    for n in range(7):
+        near_merge(n).wait()
+    tile = M1[h, y, s]
+    for n in range(7):
+        tile = tile + MN[n]
+    OT[...] = tile
     g_end(first)
 
     for part in (first, second):
         for k in (1, 2, 3):
-            w_team(part, k).wait_send()
             g_t(part, k).wait_send()
         for c in range(part.chunks):
             w_h(part, c).wait_send()
@@ -1224,17 +1328,23 @@
             for n in range(4):
                 w_s(part, c, n // 2, n % 2).wait_send()
     for i in range(8):
-        share_copy(i, 1 - s).wait_send()
+        for slot in range(4):
+            share_copy(i, 1 - s, slot).wait_send()
     remote(XIN.at[1], lo.at[1 - s], ss_o.at[0], rs_o.at[0], sib).wait()
-    remote(OWN, ig.at[1 - s], ss_o.at[1], rs_o.at[1], sib).wait_recv()
-
-
-def finish_kernel(lo_in, ig_in, OQ, OO, OU, OD, OT, half, lo, ig, oq, oo, ou, od, a0, a1, a2, a3, a4, bu, a5, tab):
-    lo[...] = lo_in[...]
-    ig[...] = ig_in[...]
-    oo[...] = OO[...]
-    od[...] = OD[...]
-    block = OD.shape[0]
+    remote(DX, ig.at[1 - s], ss_o.at[1], rs_o.at[1], sib).wait()
+
+
+def finish_kernel(
+    lo_in, ig_in, oq_in, oo_in, ou_in, od_in, ot_in, half,
+    lo, ig, oq, oo, ou, od, a0, a1, a2, a3, a4, bu, a5, tab, OQ, OU, OT, sem,
+):
+    moves = ((oq_in, OQ), (ou_in, OU), (ot_in, OT), (lo_in, lo), (ig_in, ig), (oo_in, oo), (od_in, od))
+    moves = [pltpu.make_async_copy(a, b, sem.at[i]) for i, (a, b) in enumerate(moves)]
+    for cp in moves:
+        cp.start()
+    for cp in moves[:3]:
+        cp.wait()
+    block = od.shape[0]
     for hh in range(2):
         for zz in range(2):
             for yy in range(2):
@@ -1255,6 +1365,8 @@
         bu[:, 128 * r : 128 * r + 128] = jnp.where(x == 0, OT[6 + r : 7 + r, :], OT[8 + r : 9 + r, :])
     for b in range(2):
         tab[:, 16 * b : 16 * b + 16] = jnp.where(x == 0, OT[12 + b : 13 + b, :16], OT[14 + b : 15 + b, :16])
+    for cp in moves[3:]:
+        cp.wait()
 
 
 def vm(n=1):
@@ -1296,31 +1408,32 @@
             shape_of((block, width), F32),
             shape_of((16, 128), F32),
         ),
-        in_specs=vm(4) + hb(4) + vm(8),
+        in_specs=hb(2) + vm(2) + hb(4) + vm(8),
         out_specs=tuple(vm(7)),
         scratch_shapes=[
             low(4, part, 3 * wide), low(4, part, ff),
             low(2, 2, 2, 2, 2, part, 3 * wide), low(2, 4, part, width),
-            low(2, 2, 2, 2, 2, part, ff), low(2, 4, block, width),
-            low(3, rows, width), low(3, rows, width),
+            low(2, 2, 2, 2, 2, part, ff), low(2, 4, block, width), low(4, rows, width),
+            low(3, rows, width),
             low(2, 4, rows, width), low(2, 4, rows, width), low(2, 4, rows, ff), low(2, 4, rows, wide),
             low(2, 4, rows, 3 * wide), full(2, 4, 4 * rows, rows), full(8 * rows, ff), full(2, rows, width),
             low(2, 4, rows, width), low(2, 4, rows, width), low(2, 4, rows, ff), low(2, 4, rows, 3 * wide),
             low(4, rows, width), low(4, rows, width), low(4, rows, ff), low(4, rows, wide),
             low(4, rows, width), low(4, rows, width), low(4, rows, ff), low(4, rows, 3 * wide),
-            low(4, rows, width), low(4, rows, width), full(rows, width), full(rows, width),
+            low(4, rows, width), low(4, rows, width), full(rows, width),
+            full(rows, width), full(rows, width), full(rows, width),
             low(2, 2, 2, 2, part, 3 * wide), low(4, part, width), low(2, 2, 2, 2, part, ff), low(4, block, width),
             low(2, 2, 2, part, 3 * wide), low(2, part, width), low(2, 2, 2, part, ff), low(2, block, width),
             low(2, 2, part, 3 * wide), low(part, width), low(2, 2, part, ff), low(block, width),
             low(2, 2, part, 3 * wide), low(part, width), low(2, 2, part, ff), low(block, width),
-            low(4, part, 3 * wide), low(4, part, 3 * wide), low(4, part, ff), low(4, part, ff),
-            full(2, 2, 2, 2, 16, 128), full(2, 16, 128), full(2, 8, width), full(4, 8, 128),
+            low(4, part, 3 * wide), low(4, part, ff),
+            full(2, 2, 2, 2, 16, 128), full(4, 2, 2, 2, 16, 128), full(2, 8, width), full(4, 8, 128),
             full(2, 4 * rows, rows), full(128, 128), full(2, 8, width), full(2, 1, ff), full(2, 4 * rows, rows),
-            full(2, 2, 2, 2, 16, 128), full(2, 2, 2, 2, 16, 128),
-            sems(9), sems(2, 4), sems(2, 4), sems(2, 2, 4), sems(2, 2, 4), sems(2, 4), sems(2, 4),
-            sems(2, 4, 4), sems(2, 4, 4), sems(5), sems(5),
-            sems(8, 4), sems(8, 4), sems(8, 4), sems(8, 4), sems(8), sems(8), sems(2), sems(2),
-            sems(2, 2, 4), sems(2, 2, 4), sems(2, 4), sems(2, 4), sems(2, 4), sems(2, 4), sems(5), sems(5),
+            full(2, 2, 2, 2, 16, 128), full(4, 2, 2, 2, 16, 128), full(2, 2, 2, 16, 128), full(7, 16, 128),
+            sems(11), sems(2, 4), sems(2, 4), sems(2, 2, 4), sems(2, 2, 4), sems(2, 4), sems(2, 4),
+            sems(2, 4, 4), sems(2, 4, 4), sems(10), sems(10),
+            sems(8, 6), sems(8, 6), sems(8, 4), sems(8, 4), sems(8, 4), sems(8, 4), sems(2), sems(2),
+            sems(2, 2, 4), sems(2, 2, 4), sems(2, 4), sems(2, 4), sems(2, 4), sems(2, 4), sems(10), sems(10),
         ],
         compiler_params=pltpu.CompilerParams(
             collective_id=0, has_side_effects=True, vmem_limit_bytes=63 << 20
@@ -1345,9 +1458,10 @@
         )
         + (shape_of((1, part), F32),) * 5
         + (shape_of((1, block), F32), shape_of((1, part), F32), shape_of((1, 32), F32)),
-        in_specs=vm(7) + [pl.BlockSpec(memory_space=pltpu.SMEM)],
+        in_specs=hb(7) + [pl.BlockSpec(memory_space=pltpu.SMEM)],
         out_specs=tuple(vm(14)),
-        compiler_params=pltpu.CompilerParams(vmem_limit_bytes=32 << 20),
+        scratch_shapes=[full(4, part, 3 * wide), full(4, part, ff), full(16, 128), sems(7)],
+        compiler_params=pltpu.CompilerParams(vmem_limit_bytes=62 << 20),
         name="finish",
     )(lo, ig, OQ, OO, OU, OD, OT, half)
     return (

time: 309 us -> 250 us (0.81)
  Pallas kernels: 299 us -> 248 us
  local copies, waits for them, and re-layouts: 8.64 us -> 1.3 us
    pallas_call x1, Pallas kernels: 297 us -> 243 us  [team_local(): pl.pallas_call(step_kernel, out_shape=(shape_of((2, rows, width), BF), sh...]
    unnamed x17 -> x3, local copies, waits for them, and re-layouts: 8.64 us -> 1.3 us
where the time goes in v3:
time: 250 us
  Pallas kernels  248 us (99%)
    pallas_call x1, Pallas kernels, team_local(): pl.pallas_call(step_kernel, out_shape=(shape_of((2, rows, width), BF), sh...  243 us

profile of v3, /device:TPU:0, one launch (start us, length us, event | category | flops | bytes accessed | tf_op | source)
XLA Modules:
  0.0 249.9 jit_solution(9495414397794422413)
XLA Ops:
  0.7 0.0 copy-start
  0.7 0.6 copy-done
  1.3 0.6 copy.30.il_ref
  2.0 243.4 %two_layers.1 = (bf16[2,96,1024]{2,1,0:T(8,128)(2,1)}, f32[2,96,1024]{2,1,0:T(8,128)}, f32[4,64,768]{2,1,0:T(8,128)}, f32[64,1024]{1,0:T(8,128)}, f32[4,64,1024]...) custom-call(bf16[2,96,1024]{2,1,0:T(8,128)(2,1)} %bitcast.21, bf16[2,96,1024]{2,1,0:T(8,128)(2,1)} %bitcast.22, ...), custom_call_target="tpu_custom_call" | custom-call | tf_op jit(solution)/shard_map/two_layers/pallas_call | solution.py:1400
  245.4 4.4 %finish.1 = (bf16[2,96,1024]{2,1,0:T(8,128)(2,1)}, f32[2,96,1024]{2,1,0:T(8,128)}, f32[64,3072]{1,0:T(8,128)}, f32[64,1024]{1,0:T(8,128)}, f32[64,4096]{1,0:T(8,...) custom-call(bf16[2,96,1024]{2,1,0:T(8,128)(2,1)} %get-tuple-element., ...), custom_call_target="tpu_custom_call" | custom-call | tf_op jit(solution)/shard_map/finish/pallas_call | solution.py:1449
Async XLA Ops:
  0.7 0.7 copy-start

commit v4 on v3

--- a/solution.py
+++ b/solution.py
@@ -555,8 +555,8 @@
     v0_ref, v1_ref, v2_ref, v3_ref, v4_ref, v5_ref, bu_ref, rt_ref,
     lo, ig, OQ, OO, OU, OD, OT,
     SQ, SU, WQ, WO, WU, WD, XG, XIN, A, C, FA, MIX, QKV, PR, UF, HM, DZ, DAT, DU, DQ,
-    XA, XC, XF, XM, XDZ, XDAT, XDU, XDQ, RB, SB, OWN, OWNY, DX, DH,
-    GQ, GO, GU, GD, YQ, YO, YU, YD, ZSQ, ZSO, ZSU, ZSD, ZRQ, ZRO, ZRU, ZRD, TRQ, TRU,
+    XA, XC, XF, XM, XDZ, XDAT, XDU, XDQ, RB, SB, SY, RY, OWN, OWNY, DX, DH,
+    GQ, GO, YQ, YO, YU, YD, ZSQ, ZSO, ZSU, ZSD, ZRQ, ZRO, ZRU, ZRD, TRQ, TRU,
     SPT, SPR, VEC, LEN, BIAS, PD, SGV, SBU, DS, MT, MR, M1, MN,
     ls, ss_a, rs_a, ss_wy, rs_wy, ss_wh, rs_wh, ss_ws, rs_ws, ss_p, rs_p,
     ss_g, rs_g, ss_r, rs_r, ss_x, rs_x, ss_o, rs_o,
@@ -577,7 +577,6 @@
         def _():
             what()
 
-    SY, RY = DU.at[0], DAT.at[0]
     half = rows // 2
     upper, lower = pl.ds(0, half), pl.ds(half, half)
     x_dev, x_slot = p.team(1)
@@ -632,7 +631,8 @@
         @pl.when(k > 0)
         def _():
             (SY if side else SB)[k] = value.astype(BF)
-            reduce_copy(c, k, side).start()
+            if not side:
+                reduce_copy(c, k).start()
 
     def reduce_end(c, side=False):
         total = (OWNY if side else OWN)[...]
@@ -672,7 +672,7 @@
 
     first = Part(0, 1, W=WQ, V=WO, S=SQ, G=GQ, R=GO, Y=YQ, YR=YO, ZS=ZSQ, ZSR=ZSO, ZR=ZRQ, ZRR=ZRO,
                  TS=SQ, TR=TRQ, O=OQ, OR=OO)
-    second = Part(1, 2, W=WU, V=WD, S=SU, G=GU, R=GD, Y=YU, YR=YD, ZS=ZSU, ZSR=ZSD, ZR=ZRU, ZRR=ZRD,
+    second = Part(1, 2, W=WU, V=WD, S=SU, G=WU.at[1], R=WD.at[1], Y=YU, YR=YD, ZS=ZSU, ZSR=ZSD, ZR=ZRU, ZRR=ZRD,
                   TS=SU, TR=TRU, O=OU, OR=OD)
 
     loads = [
@@ -796,7 +796,7 @@
     WD[s, q] = UF[64 : 64 + block, :].astype(BF)
 
     position = lanes_of((rows, 1), 0).astype(F32)
-    count = jnp.where(s == 0, il_ref[0:1, :], il_ref[1:2, :]).astype(F32)
+    count = jnp.where(s == 0, il_ref[:, 0:1], il_ref[:, 1:2]).astype(F32)
     valid = (position < count).astype(F32)
     loads[10].wait()
     DZ[1, t] = (valid * DZ[1, t].astype(F32)).astype(BF)
@@ -809,7 +809,7 @@
         for i in range(2):
             lines.append(jnp.where(x == xx, bu_ref[:, 128 * i : 128 * i + 128], zero))
     table = jnp.concatenate([rt_ref[...], jnp.zeros((1, 96), F32)], axis=1)
-    counts = jnp.where(lane == 0, il_ref[0:1, :].astype(F32), jnp.where(lane == 1, il_ref[1:2, :].astype(F32), zero))
+    counts = jnp.where(lane == 0, il_ref[:, 0:1].astype(F32), jnp.where(lane == 1, il_ref[:, 1:2].astype(F32), zero))
     for piece in (table, counts):
         for xx in range(2):
             lines.append(jnp.where(x == xx, piece, zero))
@@ -1239,11 +1239,15 @@
     for part in (first, second):
         for k in (1, 2, 3):
             w_team(part, k).wait_send()
+        for c in range(part.chunks):
+            w_h(part, c).wait_send()
+            for n in range(2):
+                w_y(part, c, n).wait_send()
+            for n in range(4):
+                w_s(part, c, n // 2, n % 2).wait_send()
     only(1, lambda: g_make(second, 0))
     SGV[1, 5:6, :] = column_sum(DZ[1, t].astype(F32))
     middle_back(1)
-    XIN[2] = layer_result(1)
-    give_result(1)
     attention_back(1)
     only(1, lambda: g_make(first, 0))
     inputs_back(1)
@@ -1253,10 +1257,11 @@
     only(1, lambda: g_total(second))
     middle_back(0)
     attention_back(0)
-    only(0, lambda: (g_make(first, 0), g_make(first, 1)))
+    for k in (1, 2, 3):
+        reduce_copy(3, k, True).start()
+    only(0, lambda: (g_make(first, 0), g_fold(first, 2), g_make(first, 1)))
+    only(0, lambda: (g_fold(first, 0), g_fold(first, 1), g_later(first)))
     inputs_back(0)
-
-    only(0, lambda: (g_fold(first, 2), g_fold(first, 0), g_fold(first, 1), g_later(first)))
 
     spread = []
     for i in range(2):
@@ -1306,6 +1311,8 @@
         M1[hh] = MT[hh, z] + MR[1, hh] + MR[2, hh] + MR[3, hh]
     for n in range(7):
         near_merge(n).start()
+    XIN[2] = layer_result(1)
+    give_result(1)
     g_total(first)
     g_end(second)
     for n in range(7):
@@ -1320,13 +1327,9 @@
         for k in (1, 2, 3):
             g_t(part, k).wait_send()
         for c in range(part.chunks):
-            w_h(part, c).wait_send()
             g_h(part, c).wait_send()
             for n in range(2):
-                w_y(part, c, n).wait_send()
                 g_y(part, c, n).wait_send()
-            for n in range(4):
-                w_s(part, c, n // 2, n % 2).wait_send()
     for i in range(8):
         for slot in range(4):
             share_copy(i, 1 - s, slot).wait_send()
@@ -1335,7 +1338,7 @@
 
 
 def finish_kernel(
-    lo_in, ig_in, oq_in, oo_in, ou_in, od_in, ot_in, half,
+    lo_in, ig_in, oq_in, oo_in, ou_in, od_in, ot_in,
     lo, ig, oq, oo, ou, od, a0, a1, a2, a3, a4, bu, a5, tab, OQ, OU, OT, sem,
 ):
     moves = ((oq_in, OQ), (ou_in, OU), (ot_in, OT), (lo_in, lo), (ig_in, ig), (oo_in, oo), (od_in, od))
@@ -1358,7 +1361,7 @@
                     )
                 for xx in range(2):
                     ou[:, (d + xx) * block : (d + xx + 1) * block] = OU[xx + 2 * zz, :, n * block : (n + 1) * block]
-    x = half[0]
+    x = lax.axis_index("dp") % 2
     for i, ref in enumerate((a0, a1, a2, a3, a4, a5)):
         ref[...] = jnp.where(x == 0, OT[i : i + 1, :HD], OT[i : i + 1, HD:])
     for r in range(2):
@@ -1420,9 +1423,9 @@
             low(2, 4, rows, width), low(2, 4, rows, width), low(2, 4, rows, ff), low(2, 4, rows, 3 * wide),
             low(4, rows, width), low(4, rows, width), low(4, rows, ff), low(4, rows, wide),
             low(4, rows, width), low(4, rows, width), low(4, rows, ff), low(4, rows, 3 * wide),
-            low(4, rows, width), low(4, rows, width), full(rows, width),
+            low(4, rows, width), low(4, rows, width), low(4, rows, width), low(4, rows, width), full(rows, width),
             full(rows, width), full(rows, width), full(rows, width),
-            low(2, 2, 2, 2, part, 3 * wide), low(4, part, width), low(2, 2, 2, 2, part, ff), low(4, block, width),
+            low(2, 2, 2, 2, part, 3 * wide), low(4, part, width),
             low(2, 2, 2, part, 3 * wide), low(2, part, width), low(2, 2, 2, part, ff), low(2, block, width),
             low(2, 2, part, 3 * wide), low(part, width), low(2, 2, part, ff), low(block, width),
             low(2, 2, part, 3 * wide), low(part, width), low(2, 2, part, ff), low(block, width),
@@ -1440,12 +1443,11 @@
         ),
         name="two_layers",
     )(
-        audio_in.reshape(2, rows, width), out_grad.reshape(2, rows, width), item_len, rel_bucket[None],
+        audio_in.reshape(2, rows, width), out_grad.reshape(2, rows, width), item_len.T, rel_bucket[None],
         w_qkv[0], w_out[0], w_up[0], w_down[0],
         ln1_gain, ln1_bias, ln2_gain, ln2_bias, b_out, b_down, b_up, rel_table,
     )
 
-    half = (lax.axis_index("dp") % 2).reshape(1)
     lo, ig, oq, oo, ou, od, a0, a1, a2, a3, a4, bu, a5, tab = pl.pallas_call(
         finish_kernel,
         out_shape=(
@@ -1458,12 +1460,12 @@
         )
         + (shape_of((1, part), F32),) * 5
         + (shape_of((1, block), F32), shape_of((1, part), F32), shape_of((1, 32), F32)),
-        in_specs=hb(7) + [pl.BlockSpec(memory_space=pltpu.SMEM)],
+        in_specs=hb(7),
         out_specs=tuple(vm(14)),
         scratch_shapes=[full(4, part, 3 * wide), full(4, part, ff), full(16, 128), sems(7)],
         compiler_params=pltpu.CompilerParams(vmem_limit_bytes=62 << 20),
         name="finish",
-    )(lo, ig, OQ, OO, OU, OD, OT, half)
+    )(lo, ig, OQ, OO, OU, OD, OT)
     return (
         lo[None, :, None], ig[None, :, None], oq[None], oo[None], ou[None], od[None],
         a0, a1, a2, a3, a4, bu, a5, tab,

time: 250 us -> 248 us (level)
  no operation moved by 1% of the time
where the time goes in v4:
time: 248 us
  Pallas kernels  247 us (100%)
    pallas_call x1, Pallas kernels, team_local(): pl.pallas_call(step_kernel, out_shape=(shape_of((2, rows, width), BF), sh...  243 us

profile of v4, /device:TPU:0, one launch (start us, length us, event | category | flops | bytes accessed | tf_op | source)
XLA Modules:
  0.0 248.1 jit_solution(7653343831694275085)
XLA Ops:
  0.7 242.9 %two_layers.1 = (bf16[2,96,1024]{2,1,0:T(8,128)(2,1)}, f32[2,96,1024]{2,1,0:T(8,128)}, f32[4,64,768]{2,1,0:T(8,128)}, f32[64,1024]{1,0:T(8,128)}, f32[4,64,1024]...) custom-call(bf16[2,96,1024]{2,1,0:T(8,128)(2,1)} %bitcast.21, bf16[2,96,1024]{2,1,0:T(8,128)(2,1)} %bitcast.22, ...), custom_call_target="tpu_custom_call" | custom-call | tf_op jit(solution)/shard_map/two_layers/pallas_call | solution.py:1403
  243.5 4.4 %finish.1 = (bf16[2,96,1024]{2,1,0:T(8,128)(2,1)}, f32[2,96,1024]{2,1,0:T(8,128)}, f32[64,3072]{1,0:T(8,128)}, f32[64,1024]{1,0:T(8,128)}, f32[64,4096]{1,0:T(8,...) custom-call(bf16[2,96,1024]{2,1,0:T(8,128)(2,1)} %get-tuple-element., ...), custom_call_target="tpu_custom_call" | custom-call | tf_op jit(solution)/shard_map/finish/pallas_call | solution.py:1451

commit v5 on v4

--- a/solution.py
+++ b/solution.py
@@ -1172,13 +1172,13 @@
     def middle_back(layer):
         dc = reduce_end(6 - 2 * layer)
         normed, scale = rows_norm(HM[layer])
-        SGV[layer, 2:3, :] = column_sum(dc * normed)
-        SGV[layer, 3:4, :] = column_sum(dc)
         dh = DZ[layer, t].astype(F32) + norm_back(dc, normed, scale, row(layer, 2))
         DH[...] = dh
         dattn = dh.astype(BF)
         DAT[layer, t] = dattn
         gather_start(DAT.at[layer], 7 - 2 * layer)
+        SGV[layer, 2:3, :] = column_sum(dc * normed)
+        SGV[layer, 3:4, :] = column_sum(dc)
         SGV[layer, 4:5, :] = column_sum(dattn.astype(F32))
         only(layer, lambda: (g_make(second, 1), g_fold(second, 0), g_fold(second, 1)))
 
@@ -1257,8 +1257,6 @@
     only(1, lambda: g_total(second))
     middle_back(0)
     attention_back(0)
-    for k in (1, 2, 3):
-        reduce_copy(3, k, True).start()
     only(0, lambda: (g_make(first, 0), g_fold(first, 2), g_make(first, 1)))
     only(0, lambda: (g_fold(first, 0), g_fold(first, 1), g_later(first)))
     inputs_back(0)
@@ -1304,6 +1302,8 @@
 
     for k in (1, 2, 3):
         team_merge(k).start()
+    for k in (1, 2, 3):
+        reduce_copy(3, k, True).start()
     only(0, lambda: g_total(second))
     for k in (1, 2, 3):
         team_merge(k).wait()
@@ -1311,10 +1311,10 @@
         M1[hh] = MT[hh, z] + MR[1, hh] + MR[2, hh] + MR[3, hh]
     for n in range(7):
         near_merge(n).start()
+    g_total(first)
+    g_end(second)
     XIN[2] = layer_result(1)
     give_result(1)
-    g_total(first)
-    g_end(second)
     for n in range(7):
         near_merge(n).wait()
     tile = M1[h, y, s]
@@ -1339,28 +1339,45 @@
 
 def finish_kernel(
     lo_in, ig_in, oq_in, oo_in, ou_in, od_in, ot_in,
-    lo, ig, oq, oo, ou, od, a0, a1, a2, a3, a4, bu, a5, tab, OQ, OU, OT, sem,
+    lo, ig, oq, oo, ou, od, a0, a1, a2, a3, a4, bu, a5, tab,
+    OQ, OU, OT, LO, IG, OO, OD, FQ, FU, came, left,
 ):
-    moves = ((oq_in, OQ), (ou_in, OU), (ot_in, OT), (lo_in, lo), (ig_in, ig), (oo_in, oo), (od_in, od))
-    moves = [pltpu.make_async_copy(a, b, sem.at[i]) for i, (a, b) in enumerate(moves)]
+    moves = ((oq_in, OQ), (ou_in, OU), (ot_in, OT), (ig_in, IG), (od_in, OD), (lo_in, LO), (oo_in, OO))
+    moves = [pltpu.make_async_copy(a, b, came.at[i]) for i, (a, b) in enumerate(moves)]
     for cp in moves:
         cp.start()
-    for cp in moves[:3]:
-        cp.wait()
-    block = od.shape[0]
+    block = OD.shape[0]
+    outs = []
+
+    def leave(src, dst):
+        cp = pltpu.make_async_copy(src, dst, left.at[len(outs)])
+        cp.start()
+        outs.append(cp)
+
+    moves[0].wait()
     for hh in range(2):
         for zz in range(2):
             for yy in range(2):
-                n = 2 * hh + yy
-                d = 2 * yy + 4 * zz + 8 * hh
                 for i in range(3):
-                    at = i * 4 * HD + n * HD
-                    to = i * 16 * HD + d * HD
-                    oq[:, to : to + 2 * HD] = jnp.concatenate(
+                    at = (4 * i + 2 * hh + yy) * HD
+                    to = (16 * i + 2 * yy + 4 * zz + 8 * hh) * HD
+                    FQ[:, to : to + 2 * HD] = jnp.concatenate(
                         [OQ[2 * zz, :, at : at + HD], OQ[2 * zz + 1, :, at : at + HD]], axis=1
                     )
+    leave(FQ, oq)
+    moves[1].wait()
+    for hh in range(2):
+        for zz in range(2):
+            for yy in range(2):
                 for xx in range(2):
-                    ou[:, (d + xx) * block : (d + xx + 1) * block] = OU[xx + 2 * zz, :, n * block : (n + 1) * block]
+                    n = 2 * hh + yy
+                    d = xx + 2 * yy + 4 * zz + 8 * hh
+                    FU[:, d * block : (d + 1) * block] = OU[xx + 2 * zz, :, n * block : (n + 1) * block]
+    leave(FU, ou)
+    for i, (src, dst) in enumerate(((IG, ig), (OD, od), (LO, lo), (OO, oo))):
+        moves[3 + i].wait()
+        leave(src, dst)
+    moves[2].wait()
     x = lax.axis_index("dp") % 2
     for i, ref in enumerate((a0, a1, a2, a3, a4, a5)):
         ref[...] = jnp.where(x == 0, OT[i : i + 1, :HD], OT[i : i + 1, HD:])
@@ -1368,7 +1385,7 @@
         bu[:, 128 * r : 128 * r + 128] = jnp.where(x == 0, OT[6 + r : 7 + r, :], OT[8 + r : 9 + r, :])
     for b in range(2):
         tab[:, 16 * b : 16 * b + 16] = jnp.where(x == 0, OT[12 + b : 13 + b, :16], OT[14 + b : 15 + b, :16])
-    for cp in moves[3:]:
+    for cp in outs:
         cp.wait()
 
 
@@ -1461,8 +1478,12 @@
         + (shape_of((1, part), F32),) * 5
         + (shape_of((1, block), F32), shape_of((1, part), F32), shape_of((1, 32), F32)),
         in_specs=hb(7),
-        out_specs=tuple(vm(14)),
-        scratch_shapes=[full(4, part, 3 * wide), full(4, part, ff), full(16, 128), sems(7)],
+        out_specs=tuple(hb(6) + vm(8)),
+        scratch_shapes=[
+            full(4, part, 3 * wide), full(4, part, ff), full(16, 128),
+            low(2, rows, width), full(2, rows, width), full(part, width), full(block, width),
+            full(part, 3 * width), full(part, hidden), sems(7), sems(6),
+        ],
         compiler_params=pltpu.CompilerParams(vmem_limit_bytes=62 << 20),
         name="finish",
     )(lo, ig, OQ, OO, OU, OD, OT)

time: 248 us -> 248 us (level)
  no operation moved by 1% of the time
where the time goes in v5:
time: 248 us
  Pallas kernels  247 us (100%)
    pallas_call x1, Pallas kernels, team_local(): pl.pallas_call(step_kernel, out_shape=(shape_of((2, rows, width), BF), sh...  243 us

profile of v5, /device:TPU:0, one launch (start us, length us, event | category | flops | bytes accessed | tf_op | source)
XLA Modules:
  0.0 247.9 jit_solution(919502266996715024)
XLA Ops:
  0.7 242.9 %two_layers.1 = (bf16[2,96,1024]{2,1,0:T(8,128)(2,1)}, f32[2,96,1024]{2,1,0:T(8,128)}, f32[4,64,768]{2,1,0:T(8,128)}, f32[64,1024]{1,0:T(8,128)}, f32[4,64,1024]...) custom-call(bf16[2,96,1024]{2,1,0:T(8,128)(2,1)} %bitcast.21, bf16[2,96,1024]{2,1,0:T(8,128)(2,1)} %bitcast.22, ...), custom_call_target="tpu_custom_call" | custom-call | tf_op jit(solution)/shard_map/two_layers/pallas_call | solution.py:1420
  243.6 4.1 %finish.1 = (bf16[2,96,1024]{2,1,0:T(8,128)(2,1)}, f32[2,96,1024]{2,1,0:T(8,128)}, f32[64,3072]{1,0:T(8,128)}, f32[64,1024]{1,0:T(8,128)}, f32[64,4096]{1,0:T(8,...) custom-call(bf16[2,96,1024]{2,1,0:T(8,128)(2,1)} %get-tuple-element., ...), custom_call_target="tpu_custom_call" | custom-call | tf_op jit(solution)/shard_map/finish/pallas_call | solution.py:1468
